TPU v7x, 32 devices: a whole 2x2x4 slice. The times are simulated.
32 devices in a mesh: dp: 8 (over y, x, core), seq: 4 (over z).
Axes of the slice: x: 2, y: 2, z: 4, core: 2. Of those that a mesh axis runs over, the one named last changes fastest.
Arguments:
- tokens: bfloat16 [24, 1024, 768], P('dp', 'seq'), may hold values from -6 to 6
- lengths: int32 [24], P('dp'), may hold values from 256 to 1024, as said below
- query_weight: float32 [768, 768], P('dp'), may hold values from -0.3125 to 0.3125
- query_shift: float32 [768], P('dp'), may hold values from -3 to 3
- key_weight: float32 [768, 768], P('dp'), may hold values from -0.3125 to 0.3125
- value_weight: float32 [768, 768], P('dp'), may hold values from -0.21875 to 0.21875
- value_shift: float32 [768], P('dp'), may hold values from -3 to 3
- merge_weight: float32 [768, 768], P('dp'), may hold values from -0.875 to 0.875
- merge_shift: float32 [768], P('dp'), may hold values from -3 to 3
- first_gain: float32 [768], P('dp'), may hold values from 0.1 to 1.9
- first_shift: float32 [768], P('dp'), may hold values from -3 to 3
- expand_weight: float32 [768, 3072], P('dp'), may hold values from -0.21875 to 0.21875
- expand_shift: float32 [3072], P('dp'), may hold values from -3 to 3
- reduce_weight: float32 [3072, 768], P('dp'), may hold values from -0.15625 to 0.15625
- reduce_shift: float32 [768], P('dp'), may hold values from -3 to 3
- second_gain: float32 [768], P('dp'), may hold values from 0.1 to 1.9
- second_shift: float32 [768], P('dp'), may hold values from -3 to 3
- upstream: bfloat16 [24, 1024, 768], P('dp', 'seq'), may hold values from -6 to 6
Outputs:
- output: bfloat16 [24, 1024, 768], P('dp', 'seq')
- token_grad: bfloat16 [24, 1024, 768], P('dp', 'seq')
- dquery_weight: float32 [768, 768], P('dp')
- dquery_shift: float32 [768], P('dp')
- dkey_weight: float32 [768, 768], P('dp')
- dvalue_weight: float32 [768, 768], P('dp')
- dvalue_shift: float32 [768], P('dp')
- dmerge_weight: float32 [768, 768], P('dp')
- dmerge_shift: float32 [768], P('dp')
- dfirst_gain: float32 [768], P('dp')
- dfirst_shift: float32 [768], P('dp')
- dexpand_weight: float32 [768, 3072], P('dp')
- dexpand_shift: float32 [3072], P('dp')
- dreduce_weight: float32 [3072, 768], P('dp')
- dreduce_shift: float32 [768], P('dp')
- dsecond_gain: float32 [768], P('dp')
- dsecond_shift: float32 [768], P('dp')
Inputs may be any that keep to these rules, and one draw needn't show every extreme that they name: `lengths`: the valid length of each sequence; keys at this position or later are masked out.
All inputs are finite; a program needn't handle non-finite values.
Results may differ from a plain program's by a relative error of at most 0.018.
The roundings to bfloat16 on the way count: a program that leaves them out, or rounds other values in their place, can miss the bound.
Values may be sent and summed in bfloat16 or wider, within the bound.
A program may use at most 192 MiB of HBM per device.

v0:
```python
import functools

import jax
import jax.numpy as jnp
from jax import lax
from jax.experimental import pallas as pl
from jax.experimental.pallas import tpu as pltpu
from jax.sharding import PartitionSpec as P

HEAD = 64
LANES = 128
EPS = 1e-12
NEG_FILL = -1000000000.0
SCALE2 = 0.125 * 1.4426950408889634
F32 = jnp.float32
BF16 = jnp.bfloat16
VMEM_LIMIT = 60 * 1024 * 1024
VMEM_MAX = 67043328


def dot(left, right, left_dim, right_dim):
    return lax.dot_general(
        left, right, (((left_dim,), (right_dim,)), ((), ())), preferred_element_type=F32
    )


def attend_kernel(bias_ref, q_ref, k_ref, v_ref, ctx_ref, probs_ref, *, rows_blk):
    seq_len = q_ref.shape[0]
    lane = lax.broadcasted_iota(jnp.int32, (1, LANES), 1)
    bias = bias_ref[...]
    for blk in range(seq_len // rows_blk):
        rows = pl.ds(blk * rows_blk, rows_blk)
        query = q_ref[rows, :]
        mixed = []
        for head in range(2):
            mine = (lane < HEAD) if head == 0 else (lane >= HEAD)
            query_h = jnp.where(mine, query, jnp.zeros_like(query))
            score = dot(query_h, k_ref[...], 1, 1) + bias
            top = jnp.max(score, axis=1, keepdims=True)
            expo = jnp.exp2((score - top) * SCALE2)
            total = jnp.sum(expo, axis=1, keepdims=True)
            probs = (expo * (1.0 / total)).astype(BF16)
            probs_ref[head, rows, :] = probs
            mixed.append(dot(probs, v_ref[...], 1, 0))
        ctx_ref[rows, :] = jnp.where(lane < HEAD, mixed[0], mixed[1]).astype(BF16)


def attend(bias, query, key, value):
    seq_len, feats = query.shape
    cols = pl.BlockSpec((seq_len, LANES), lambda g: (0, g))
    return pl.pallas_call(
        functools.partial(attend_kernel, rows_blk=min(512, seq_len)),
        grid=(feats // LANES,),
        in_specs=[pl.BlockSpec((1, seq_len), lambda g: (0, 0)), cols, cols, cols],
        out_specs=[cols, pl.BlockSpec((2, seq_len, seq_len), lambda g: (g, 0, 0))],
        out_shape=[
            jax.ShapeDtypeStruct((seq_len, feats), BF16),
            jax.ShapeDtypeStruct((feats // HEAD, seq_len, seq_len), BF16),
        ],
        compiler_params=pltpu.CompilerParams(vmem_limit_bytes=VMEM_LIMIT),
    )(bias, query, key, value)


def attend_back_pair(
    q_ref, k_ref, v_ref, ctx_ref, grad_ref, probs_ref, store, key_acc, value_acc, rows_blk
):
    seq_len = q_ref.shape[0]
    lane = lax.broadcasted_iota(jnp.int32, (1, LANES), 1)
    for blk in range(seq_len // rows_blk):
        rows = pl.ds(blk * rows_blk, rows_blk)
        query = q_ref[rows, :]
        grad = grad_ref[rows, :]
        overlap = ctx_ref[rows, :].astype(F32) * grad.astype(F32)
        query_t = query.T
        grad_t = grad.T
        grad_query = []
        for head in range(2):
            mine = (lane < HEAD) if head == 0 else (lane >= HEAD)
            part = slice(head * HEAD, (head + 1) * HEAD)
            grad_h = jnp.where(mine, grad, jnp.zeros_like(grad))
            inner = jnp.sum(jnp.where(mine, overlap, 0.0), axis=1, keepdims=True)
            probs = probs_ref[head, rows, :]
            grad_probs = dot(grad_h, v_ref[...], 1, 1)
            grad_score = (probs.astype(F32) * (grad_probs - inner)).astype(BF16)
            grad_query.append(dot(grad_score, k_ref[...], 1, 0))
            grad_key = dot(query_t[part], grad_score, 1, 0)
            grad_value = dot(grad_t[part], probs, 1, 0)
            if blk == 0:
                key_acc[head] = grad_key
                value_acc[head] = grad_value
            else:
                key_acc[head] += grad_key
                value_acc[head] += grad_value
        mixed = jnp.where(lane < HEAD, grad_query[0], grad_query[1])
        store(0, rows, (0.125 * mixed).astype(BF16))
    everything = pl.ds(0, seq_len)
    grad_key = jnp.concatenate([key_acc[0], key_acc[1]], axis=0)
    store(1, everything, (0.125 * grad_key).T.astype(BF16))
    grad_value = jnp.concatenate([value_acc[0], value_acc[1]], axis=0)
    store(2, everything, grad_value.T.astype(BF16))


def attend_back_kernel(
    q_ref, k_ref, v_ref, ctx_ref, grad_ref, probs_ref, out_ref, key_acc, value_acc, *, rows_blk
):
    def store(which, rows, values):
        out_ref[which, rows, :] = values

    attend_back_pair(
        q_ref, k_ref, v_ref, ctx_ref, grad_ref, probs_ref, store, key_acc, value_acc, rows_blk
    )


def attend_back(query, key, value, ctx, grad_ctx, probs):
    seq_len, feats = ctx.shape
    cols = pl.BlockSpec((seq_len, LANES), lambda g: (0, g))
    return pl.pallas_call(
        functools.partial(attend_back_kernel, rows_blk=min(512, seq_len)),
        grid=(feats // LANES,),
        in_specs=[cols] * 5 + [pl.BlockSpec((2, seq_len, seq_len), lambda g: (g, 0, 0))],
        out_specs=pl.BlockSpec((3, seq_len, LANES), lambda g: (0, 0, g)),
        out_shape=jax.ShapeDtypeStruct((3, seq_len, feats), BF16),
        scratch_shapes=[pltpu.VMEM((2, HEAD, seq_len), F32)] * 2,
        compiler_params=pltpu.CompilerParams(vmem_limit_bytes=VMEM_LIMIT),
    )(query, key, value, ctx, grad_ctx, probs)


MESH = pl.DeviceIdType.MESH


def remote(src, dst, send, recv, device):
    return pltpu.make_async_remote_copy(
        src_ref=src, dst_ref=dst, send_sem=send, recv_sem=recv,
        device_id=device, device_id_type=MESH,
    )


class Place:
    def __init__(self, seq_size, seq_count):
        self.me = me = lax.axis_index("dp")
        self.here = here = lax.axis_index("seq")
        core, x_at, y_at = me % 2, (me // 2) % 2, (me // 4) % 2
        self.to_core, self.to_x, self.to_y = 1 - 2 * core, 2 - 4 * x_at, 4 - 8 * y_at
        self.core_dev = (me + self.to_core, here)
        self.x_dev = (me + self.to_x, here)
        self.y_dev = (me + self.to_y, here)
        self.shift = (seq_size - seq_count) * core
        self.my_seq = here - self.shift
        self.is_owner = (self.my_seq >= 0) & (self.my_seq < seq_count)
        self.seq_size, self.seq_count = seq_size, seq_count

    def barrier(self):
        barrier = pltpu.get_barrier_semaphore()
        for device in (self.core_dev, self.x_dev, self.y_dev):
            pl.semaphore_signal(barrier, inc=1, device_id=device, device_id_type=MESH)
        for step in range(1, self.seq_size):
            pl.semaphore_signal(
                barrier, inc=1, device_id=(self.me, (self.here + step) % self.seq_size),
                device_id_type=MESH,
            )
        pl.semaphore_wait(barrier, 3 + self.seq_size - 1)


class Gather:
    def __init__(self, place, full, own, sems, index):
        self.place, self.full, self.own, self.index = place, full, own, index
        self.send_sem, self.recv_sem, self.core_send, self.core_recv = sems

    def half(self, which):
        count = self.full.shape[1] // 2
        return pl.ds(which * count, count)

    def piece(self, p):
        at = self.place
        rows = self.half(p % 2)
        shard = at.me + (0, 0, 0, 0, at.to_x, at.to_y)[p]
        src = self.own.at[rows] if p < 4 else self.full.at[shard, rows]
        device = (at.x_dev, at.y_dev, at.y_dev, at.x_dev, at.y_dev, at.x_dev)[p]
        return remote(
            src, self.full.at[shard, rows],
            self.send_sem.at[self.index, p], self.recv_sem.at[self.index, p], device,
        )

    def core_piece(self, p):
        at = self.place
        if p == 6:
            src, dst = self.own, self.full.at[at.me]
        else:
            across = at.to_x + at.to_y
            shard = at.me + (at.to_x, at.to_y, at.to_y, at.to_x, across, across)[p]
            src = dst = self.full.at[shard, self.half(p % 2)]
        return remote(
            src, dst, self.core_send.at[self.index, p], self.core_recv.at[self.index, p],
            at.core_dev,
        )

    def start(self, *pieces):
        for p in pieces:
            self.piece(p).start()

    def arrive(self, *pieces):
        for p in pieces:
            self.piece(p).wait_recv()

    def to_core(self, *pieces):
        for p in pieces:
            self.core_piece(p).start()

    def finish(self, pieces, core_pieces):
        for p in core_pieces:
            self.core_piece(p).wait_recv()
        for p in pieces:
            self.piece(p).wait_send()
        for p in core_pieces:
            self.core_piece(p).wait_send()


class RowsIn:
    def __init__(self, place, blocks, whole, buf, sems):
        self.place, self.blocks, self.whole, self.buf = place, blocks, whole, buf
        self.send_sem, self.recv_sem, self.local_sem = sems
        self.rows = blocks.shape[1]

    def to(self, seq, source):
        at = self.place
        return remote(
            self.blocks.at[seq], self.whole.at[pl.ds(source * self.rows, self.rows)],
            self.send_sem.at[seq], self.recv_sem.at[source], (at.me, seq + at.shift),
        )

    def own(self, count):
        at = self.place

        def out(pos, k):
            return pltpu.make_async_copy(
                self.buf, self.whole.at[pl.ds(pos * self.rows, self.rows)], self.local_sem.at[k]
            )

        @pl.when(at.is_owner)
        def _():
            load = pltpu.make_async_copy(self.blocks.at[at.my_seq], self.buf, self.local_sem.at[0])
            load.start()
            load.wait()
            out(at.here, 1).start()
            out(at.here, 1).wait()

        @pl.when(jnp.logical_not(at.is_owner))
        def _():
            self.buf[...] = jnp.zeros_like(self.buf)
            for pos in range(at.seq_size):
                out(pos, pos).start()
            for pos in range(at.seq_size):
                out(pos, pos).wait()

    def start(self):
        at = self.place
        for seq in range(at.seq_count):

            @pl.when(at.here != seq + at.shift)
            def _():
                self.to(seq, at.here).start()

    def finish(self):
        at = self.place

        @pl.when(at.is_owner)
        def _():
            for pos in range(at.seq_size):

                @pl.when(at.here != pos)
                def _():
                    remote(
                        self.blocks.at[0], self.whole.at[pl.ds(pos * self.rows, self.rows)],
                        self.send_sem.at[0], self.recv_sem.at[pos],
                        (at.me, (at.here + 1) % at.seq_size),
                    ).wait_recv()

        for seq in range(at.seq_count):

            @pl.when(at.here != seq + at.shift)
            def _():
                self.to(seq, at.here).wait_send()


def start_kernel(
    seq_size, seq_count, tokens, wq, wk, wv, vecs, w2, w1, wo,
    rows_out, qkv_full, vec_full, w2_full, w1_full, wo_full,
    qkv_low, w2_low, w1_low, wo_low, row_buf,
    row_send, row_recv, row_local, sem_a, sem_b, sem_c, sem_d, own_sem,
):
    place = Place(seq_size, seq_count)
    sems = (sem_a, sem_b, sem_c, sem_d)
    rows = RowsIn(place, tokens, rows_out, row_buf, (row_send, row_recv, row_local))
    first = [
        Gather(place, qkv_full, qkv_low, sems, 0),
        Gather(place, vec_full, vecs, sems, 1),
    ]
    later = [
        Gather(place, w2_full, w2_low, sems, 2),
        Gather(place, w1_full, w1_low, sems, 3),
        Gather(place, wo_full, wo_low, sems, 4),
    ]
    place.barrier()
    rows.start()
    feats = wq.shape[1]
    for k, item in enumerate((wq, wk, wv)):
        qkv_low[:, k * feats : (k + 1) * feats] = item[...].astype(BF16)
    for item in first:
        item.start(0, 1)
    for item in first:
        item.start(2, 3)
        item.to_core(6)
    w2_low[...] = w2[...].astype(BF16)
    w1_low[...] = w1[...].astype(BF16)
    wo_low[...] = wo[...].astype(BF16)
    keep = [
        pltpu.make_async_copy(item.own, item.full.at[place.me], own_sem.at[item.index])
        for item in first + later
    ]
    for copy in keep:
        copy.start()
    for item in first:
        item.arrive(0, 1)
        item.start(4, 5)
        item.to_core(0, 1)
    for item in later:
        item.start(0, 1)
    rows.own(seq_size)
    for item in first:
        item.arrive(2, 3)
        item.to_core(2, 3)
    for item in first:
        item.arrive(4, 5)
        item.to_core(4, 5)
    for item in first:
        item.finish(range(6), range(7))
    for item in later:
        item.arrive(0, 1)
        for p in (0, 1):
            item.piece(p).wait_send()
    for copy in keep:
        copy.wait()
    rows.finish()


def start_all(seq_size, tokens, qkv_parts, vecs, w2, w1, wo):
    seq_count, blk, feats = tokens.shape
    any_spec = pl.BlockSpec(memory_space=pl.ANY)
    vmem_spec = pl.BlockSpec(memory_space=pltpu.VMEM)
    dma = pltpu.SemaphoreType.DMA
    shard = qkv_parts[0].shape[0]

    def full(rows, cols):
        return jax.ShapeDtypeStruct((8, rows, cols), BF16)

    return pl.pallas_call(
        functools.partial(start_kernel, seq_size, seq_count),
        in_specs=[any_spec] + [vmem_spec] * 7,
        out_specs=[any_spec] * 6,
        out_shape=[
            jax.ShapeDtypeStruct((seq_size * blk, feats), BF16),
            full(shard, 3 * feats), full(*vecs.shape), full(*w2.shape), full(*w1.shape),
            full(*wo.shape),
        ],
        scratch_shapes=[
            pltpu.VMEM((shard, 3 * feats), BF16), pltpu.VMEM(w2.shape, BF16),
            pltpu.VMEM(w1.shape, BF16), pltpu.VMEM(wo.shape, BF16), pltpu.VMEM((blk, feats), BF16),
            dma((seq_count,)), dma((seq_size,)), dma((seq_size,)),
            dma((5, 6)), dma((5, 6)), dma((5, 7)), dma((5, 7)), dma((5,)),
        ],
        compiler_params=pltpu.CompilerParams(
            collective_id=2, has_side_effects=True, vmem_limit_bytes=VMEM_LIMIT
        ),
    )(tokens, *qkv_parts, vecs, w2, w1, wo)


def forward_kernel(
    seq_size, seq_count, rows_blk,
    bias_ref, x_ref, wq_ref, wk_ref, wv_ref, bq_ref, bv_ref, upstream, w2_in, w1_in, wo_in,
    q_ref, k_ref, v_ref, ctx_ref, probs_ref, dy_out, w2_full, w1_full, wo_full,
    row_buf, row_send, row_recv, row_local, sem_a, sem_b, sem_c, sem_d,
):
    step = pl.program_id(0)
    last = pl.num_programs(0) - 1
    place = Place(seq_size, seq_count)
    sems = (sem_a, sem_b, sem_c, sem_d)
    rows = RowsIn(place, upstream, dy_out, row_buf, (row_send, row_recv, row_local))
    later = [
        Gather(place, full, full.at[place.me], sems, k)
        for k, full in enumerate((w2_full, w1_full, wo_full))
    ]

    @pl.when(step == 0)
    def _():
        place.barrier()
        for item in later:
            item.start(2, 3)
        for item in later:
            item.start(4, 5)
        rows.start()
        for item in later:
            item.to_core(6, 0, 1)
        rows.own(seq_size)

    x_rows = x_ref[...]
    depth = x_rows.shape[1]
    mats = [ref[...].reshape(depth, LANES) for ref in (wq_ref, wk_ref, wv_ref)]
    both = dot(x_rows, jnp.concatenate(mats, axis=1), 1, 0)
    q_ref[...] = (both[:, :LANES] + bq_ref[...]).astype(BF16)
    k_ref[...] = both[:, LANES : 2 * LANES].astype(BF16)
    v_ref[...] = (both[:, 2 * LANES :] + bv_ref[...]).astype(BF16)
    attend_kernel(bias_ref, q_ref, k_ref, v_ref, ctx_ref, probs_ref, rows_blk=rows_blk)

    @pl.when(step == last - 1)
    def _():
        for item in later:
            item.arrive(2, 3)
            item.to_core(2, 3)

    @pl.when(step == last)
    def _():
        for item in later:
            item.arrive(4, 5)
            item.to_core(4, 5)
        for item in later:
            item.finish(range(2, 6), range(7))
        rows.finish()


def forward_all(seq_size, bias, rows, qkv_full, bq, bv, upstream, w2_full, w1_full, wo_full):
    seq_len, feats = rows.shape
    seq_count, blk, _ = upstream.shape
    pairs = feats // LANES
    shard = qkv_full.shape[1]
    any_spec = pl.BlockSpec(memory_space=pl.ANY)
    dma = pltpu.SemaphoreType.DMA
    cols = pl.BlockSpec((seq_len, LANES), lambda g: (0, g))

    def mat(which):
        return pl.BlockSpec((8, shard, LANES), lambda g, w=which: (0, 0, w * pairs + g))

    vec = pl.BlockSpec((1, LANES), lambda g: (0, g))
    fulls = [w2_full, w1_full, wo_full]
    flat = jax.ShapeDtypeStruct((seq_len, feats), BF16)
    return pl.pallas_call(
        functools.partial(forward_kernel, seq_size, seq_count, min(512, seq_len)),
        grid=(pairs,),
        in_specs=[
            pl.BlockSpec((1, seq_len), lambda g: (0, 0)),
            pl.BlockSpec((seq_len, feats), lambda g: (0, 0)),
            mat(0), mat(1), mat(2), vec, vec,
        ]
        + [any_spec] * 4,
        out_specs=[cols] * 4
        + [pl.BlockSpec((2, seq_len, seq_len), lambda g: (g, 0, 0))]
        + [any_spec] * 4,
        out_shape=[flat] * 4
        + [jax.ShapeDtypeStruct((feats // HEAD, seq_len, seq_len), BF16), flat]
        + [jax.ShapeDtypeStruct(item.shape, BF16) for item in fulls],
        scratch_shapes=[
            pltpu.VMEM((blk, feats), BF16),
            dma((seq_count,)), dma((seq_size,)), dma((seq_size,)),
            dma((3, 6)), dma((3, 6)), dma((3, 7)), dma((3, 7)),
        ],
        input_output_aliases={8: 6, 9: 7, 10: 8},
        compiler_params=pltpu.CompilerParams(
            collective_id=3, has_side_effects=True, vmem_limit_bytes=VMEM_LIMIT
        ),
    )(bias, rows, qkv_full, qkv_full, qkv_full, bq, bv, upstream, *fulls)


class Reduce:
    def __init__(self, place, source, total, bufs, sems, index):
        self.place, self.source, self.total, self.index = place, source, total, index
        self.own, self.other, self.first_x, self.first_y, self.second, self.arrived = bufs
        (
            self.own_sem, self.core_send, self.core_recv, self.one_send, self.one_recv,
            self.two_send, self.two_recv, self.z_send, self.z_recv,
        ) = sems
        at = place
        self.apart = [(r % 2) * at.to_x + (r // 2) * at.to_y for r in range(4)]
        self.rows = self.own.shape[1]
        self.half = self.rows // 2

    def keep_copy(self, r):
        return pltpu.make_async_copy(
            self.source(self.place.me + self.apart[r]), self.own.at[r],
            self.own_sem.at[self.index, r],
        )

    def core_copy(self, r):
        at = self.place
        return remote(
            self.source(at.me + at.to_core + self.apart[r]), self.other.at[r],
            self.core_send.at[self.index, r], self.core_recv.at[self.index, r], at.core_dev,
        )

    def one_copy(self, way, k):
        half = self.half
        if way == 0:
            src, dst = self.own.at[(1, 3)[k], pl.ds(0, half)], self.first_x.at[k]
        else:
            src, dst = self.own.at[(2, 3)[k], pl.ds(half, half)], self.first_y.at[k]
        return remote(
            src, dst, self.one_send.at[self.index, way, k], self.one_recv.at[self.index, way, k],
            (self.place.x_dev, self.place.y_dev)[way],
        )

    def two_copy(self, way):
        src = self.own.at[(2, 1)[way], pl.ds(way * self.half, self.half)]
        return remote(
            src, self.second.at[way], self.two_send.at[self.index, way],
            self.two_recv.at[self.index, way], (self.place.y_dev, self.place.x_dev)[way],
        )

    def z_copy(self, way, src):
        at = self.place
        return remote(
            src, self.arrived.at[way], self.z_send.at[self.index, way],
            self.z_recv.at[self.index, way], (at.me, at.here + (1, -1)[way]),
        )

    def hops(self, way):
        at = self.place
        return at.here if way == 0 else at.seq_size - 1 - at.here

    def add(self, dest, first, *others, start=0, count=None):
        count = self.rows if count is None else count

        def body(i, carry):
            to = pl.ds(pl.multiple_of(start + i * 16, 16), 16)
            frm = pl.ds(pl.multiple_of(i * 16, 16), 16)
            if len(others) == 1:
                dest[to, :] = first[to, :] + others[0][frm, :]
            else:
                value = first[to, :].astype(F32)
                for other in others:
                    value = value + other[frm, :].astype(F32)
                dest[to, :] = value.astype(dest.dtype)
            return carry

        lax.fori_loop(0, count // 16, body, 0, unroll=True)

    def begin(self):
        for r in (3, 1, 2, 0):
            self.core_copy(r).start()
            self.keep_copy(r).start()

    def core_stage(self):
        for r in (3, 1, 2, 0):
            self.keep_copy(r).wait()
            self.core_copy(r).wait_recv()
            self.add(self.own.at[r], self.own.at[r], self.other.at[r])
            if r == 3:
                self.one_copy(0, 1).start()
                self.one_copy(1, 1).start()
            elif r == 1:
                self.one_copy(0, 0).start()
            elif r == 2:
                self.one_copy(1, 0).start()

    def one_stage(self):
        firsts = (self.first_x, self.first_y)
        for k in (1, 0):
            for way in range(2):
                self.one_copy(way, k).wait_recv()
                dest = self.own.at[(2, 1)[way] if k else 0]
                self.add(dest, dest, firsts[way].at[k], start=way * self.half, count=self.half)
                if k:
                    self.two_copy(way).start()

    def two_stage(self):
        mine = self.own.at[0]
        for way in range(2):
            self.two_copy(way).wait_recv()
            self.add(mine, mine, self.second.at[way], start=way * self.half, count=self.half)
        self.z_hop(0)

    def z_hop(self, hop):
        mine = self.own.at[0]
        for way in range(2):
            passed = self.other.at[way]

            @pl.when(self.hops(way) == hop)
            def _():
                if hop == 0:
                    self.z_copy(way, mine).start()
                else:
                    self.z_copy(way, passed).wait_recv()
                    if hop < self.place.seq_size - 1:
                        self.add(passed, mine, self.arrived.at[way])
                        self.z_copy(way, passed).start()

    def finish(self):
        total = self.own.at[3]
        last = self.place.seq_size - 1
        mine = self.own.at[0]
        up, down = self.arrived.at[0], self.arrived.at[1]
        here = self.place.here
        self.one_copy(0, 1).wait_send()
        self.one_copy(1, 1).wait_send()

        @pl.when(here == 0)
        def _():
            self.add(total, mine, down)

        @pl.when(here == last)
        def _():
            self.add(total, mine, up)

        @pl.when((here > 0) & (here < last))
        def _():
            self.add(total, mine, up, down)

        self.total_copy().start()

    def total_copy(self):
        return pltpu.make_async_copy(
            self.own.at[3], self.total, self.own_sem.at[self.index, 3]
        )

    def drain(self):
        for r in range(4):
            self.core_copy(r).wait_send()
        for way in range(2):
            self.one_copy(way, 0).wait_send()
            self.two_copy(way).wait_send()

            @pl.when(self.hops(way) < self.place.seq_size - 1)
            def _():
                self.z_copy(way, self.own.at[0]).wait_send()

        self.total_copy().wait()

    @staticmethod
    def scratch(count, rows, width):
        return [
            pltpu.VMEM((count, lead, rows // split, width), BF16)
            for lead, split in ((4, 1), (4, 1), (2, 2), (2, 2), (2, 2), (2, 1))
        ]

    @staticmethod
    def semaphores(count):
        dma = pltpu.SemaphoreType.DMA
        return [
            dma((count, 4)), dma((count, 4)), dma((count, 4)),
            dma((count, 2, 2)), dma((count, 2, 2)), dma((count, 2)), dma((count, 2)),
            dma((count, 2)), dma((count, 2)),
        ]


class RowsOut:
    def __init__(self, place, rows, blocks, sems):
        self.place, self.rows, self.blocks = place, rows, blocks
        self.send_sem, self.recv_sem, self.local_sem = sems
        self.blk = blocks.shape[1]

    def part(self, pos):
        return self.rows.at[pl.ds(pos * self.blk, self.blk)]

    def copy(self, pos):
        at = self.place
        return remote(
            self.part(pos), self.blocks.at[at.my_seq], self.send_sem.at[pos],
            self.recv_sem.at[at.my_seq], (at.me, pos),
        )

    def keep(self, pos):
        return pltpu.make_async_copy(
            self.part(pos), self.blocks.at[self.place.my_seq], self.local_sem.at[0]
        )

    def start(self, pos):
        at = self.place

        @pl.when(at.is_owner & (at.here != pos))
        def _():
            self.copy(pos).start()

        @pl.when(at.is_owner & (at.here == pos))
        def _():
            self.keep(pos).start()

    def finish(self):
        at = self.place
        for seq in range(at.seq_count):

            @pl.when(at.here != seq + at.shift)
            def _():
                remote(
                    self.part(0), self.blocks.at[seq], self.send_sem.at[0], self.recv_sem.at[seq],
                    (at.me, (at.here + 1) % at.seq_size),
                ).wait_recv()

        @pl.when(at.is_owner)
        def _():
            self.keep(0).wait()
            for pos in range(at.seq_size):

                @pl.when(at.here != pos)
                def _():
                    self.copy(pos).wait_send()


INV_SQRT2 = 0.7071067811865476
INV_SQRT_2PI = 0.3989422804014327
BQ, BV, BO, G1, B1, C2, G2, B2, C1 = range(9)


def normalize(resid):
    centre = resid - jnp.mean(resid, axis=-1, keepdims=True)
    inv = lax.rsqrt(jnp.mean(centre * centre, axis=-1, keepdims=True) + EPS)
    return centre * inv, inv


def normalize_back(normed, inv, grad_normed):
    mean_grad = jnp.mean(grad_normed, axis=-1, keepdims=True)
    mean_both = jnp.mean(grad_normed * normed, axis=-1, keepdims=True)
    return inv * (grad_normed - mean_grad - normed * mean_both)


def gelu_parts(pre):
    cumulative = 0.5 * (1.0 + lax.erf(pre * INV_SQRT2))
    slope = cumulative + pre * (INV_SQRT_2PI * jnp.exp(-0.5 * pre * pre))
    return pre * cumulative, slope


def feed_kernel(
    rows_blk, ctx_ref, x_ref, wo_ref, vec_ref, w1_ref, w2_ref, dy_ref,
    act_ref, slope_ref, out_ref, resid_ref, normed_ref, inv_ref, vec_out,
    hidden_low,
):
    step = pl.program_id(0)
    seq_len, feats = x_ref.shape
    width = act_ref.shape[1]
    blocks = [pl.ds(i * rows_blk, rows_blk) for i in range(seq_len // rows_blk)]

    def vec(k):
        return vec_ref[k : k + 1, :]

    @pl.when(step == 0)
    def _():
        merge = wo_ref[...].reshape(feats, feats)
        for rows in blocks:
            resid = x_ref[rows, :].astype(F32) + (dot(ctx_ref[rows, :], merge, 1, 0) + vec(BO))
            normed, inv = normalize(resid)
            normed_ref[rows, :] = normed
            inv_ref[rows, :] = jnp.broadcast_to(inv, (rows_blk, LANES))
            hidden_low[rows, :] = (normed * vec(G1) + vec(B1)).astype(BF16)

    expand = w1_ref[...].reshape(feats, width)
    shrink = w2_ref[...].reshape(width, feats)
    shift = vec_ref[pl.ds(C1 + step, 1), :]
    for rows in blocks:
        act, slope = gelu_parts(dot(hidden_low[rows, :], expand, 1, 0) + shift)
        act_low = act.astype(BF16)
        act_ref[rows, :] = act_low
        slope_ref[rows, :] = slope.astype(BF16)
        part = dot(act_low, shrink, 1, 0)

        @pl.when(step == 0)
        def _():
            resid_ref[rows, :] = part

        @pl.when(step > 0)
        def _():
            resid_ref[rows, :] += part

    @pl.when(step == pl.num_programs(0) - 1)
    def _():
        sums = [jnp.zeros((1, feats), F32)] * 3
        for rows in blocks:
            hidden = normed_ref[rows, :] * vec(G1) + vec(B1)
            normed, inv = normalize(hidden + (resid_ref[rows, :] + vec(C2)))
            out_ref[rows, :] = (normed * vec(G2) + vec(B2)).astype(BF16)
            dy = dy_ref[rows, :].astype(F32)
            grad = normalize_back(normed, inv, vec(G2) * dy)
            resid_ref[rows, :] = grad
            terms = (dy * normed, dy, grad.astype(BF16).astype(F32))
            sums = [
                total + jnp.sum(term, axis=0, keepdims=True) for total, term in zip(sums, terms)
            ]
        for k, total in enumerate(sums):
            vec_out[k : k + 1, :] = total


def feed_forward(ctx, inputs, wo_full, vecs, w1_full, w2_full, dy):
    seq_len, feats = inputs.shape
    shard = w1_full.shape[1]
    hidden = w1_full.shape[2]
    steps = hidden // feats
    once = pl.Buffered(1)

    def whole(shape, mode=None):
        return pl.BlockSpec(shape, lambda j: (0,) * len(shape), pipeline_mode=mode)

    rows, rows_f32 = (seq_len, feats), jax.ShapeDtypeStruct((seq_len, feats), F32)
    cols = pl.BlockSpec(rows, lambda j: (0, j))
    wide = jax.ShapeDtypeStruct((seq_len, hidden), BF16)
    return pl.pallas_call(
        functools.partial(feed_kernel, min(256, seq_len)),
        grid=(steps,),
        in_specs=[
            whole(rows, once), whole(rows, once), whole(wo_full.shape, once),
            whole(vecs.shape, once),
            pl.BlockSpec((8, shard, feats), lambda j: (0, 0, j)),
            pl.BlockSpec((8 // steps, w2_full.shape[1], feats), lambda j: (j, 0, 0)),
            whole(rows, once),
        ],
        out_specs=[cols, cols, whole(rows), whole(rows), whole(rows), whole((seq_len, LANES)),
                   whole((8, feats))],
        out_shape=[
            wide, wide, jax.ShapeDtypeStruct(rows, BF16), rows_f32, rows_f32,
            jax.ShapeDtypeStruct((seq_len, LANES), F32), jax.ShapeDtypeStruct((8, feats), F32),
        ],
        scratch_shapes=[pltpu.VMEM(rows, BF16)],
        compiler_params=pltpu.CompilerParams(vmem_limit_bytes=VMEM_LIMIT),
    )(ctx, inputs, wo_full, vecs, w1_full, w2_full, dy)


def feed_back_kernel(seq_size, seq_count, rows_blk, *refs):
    refs = list(refs)

    def take(count):
        got = refs[:count]
        del refs[:count]
        return got

    act_ref, slope_ref, w1_ref, w2_ref, resid_ref, normed_ref, inv_ref, ctx_ref = take(8)
    wo_ref, vec_ref, vec_in, out_rows = take(4)
    d_w1, resid_out, grad_ctx, d_wo, vec_out, w2_total, out_blocks = take(7)
    grad_ffn, hidden_low, d_w2, vec_sums = take(4)
    count = 4
    bufs = take(6)
    sems = take(9)
    out_sems = take(3)

    step = pl.program_id(0)
    half_steps = pl.num_programs(0) // 2
    seq_len, feats = resid_ref.shape
    chunk = d_w2.shape[1] // count
    place = Place(seq_size, seq_count)
    outs = RowsOut(place, out_rows, out_blocks, out_sems)
    jobs = [
        Reduce(
            place, lambda shard, c=c: d_w2.at[shard, pl.ds(c * chunk, chunk)],
            w2_total.at[pl.ds(c * chunk, chunk)], [buf.at[c] for buf in bufs], sems, c,
        )
        for c in range(count)
    ]
    blocks = [pl.ds(i * rows_blk, rows_blk) for i in range(seq_len // rows_blk)]

    def vec(k):
        return vec_ref[k : k + 1, :]

    @pl.when(step == 0)
    def _():
        place.barrier()
        for pos in range(seq_size):
            outs.start(pos)
        for rows in blocks:
            grad_ffn[rows, :] = resid_ref[rows, :].astype(BF16)
            hidden_low[rows, :] = (normed_ref[rows, :] * vec(G1) + vec(B1)).astype(BF16)

    @pl.when(step < half_steps)
    def _():
        shards = 8 // half_steps
        part = dot(act_ref[...], grad_ffn[...], 0, 0).astype(BF16)
        d_w2[pl.ds(step * shards, shards)] = part.reshape(shards, d_w2.shape[1], feats)

    @pl.when(step == half_steps - 1)
    def _():
        for job in jobs:
            job.begin()

    @pl.when(step >= half_steps)
    def _():
        width = act_ref.shape[1]
        shrink = w2_ref[...].reshape(width, feats)
        expand = w1_ref[...].reshape(feats, width)
        ones = jnp.ones((8, rows_blk), BF16)
        total = jnp.zeros((8, width), F32)
        outer = jnp.zeros((feats, width), F32)
        for rows in blocks:
            grad_act = dot(grad_ffn[rows, :], shrink, 1, 1)
            grad_pre = (grad_act * slope_ref[rows, :].astype(F32)).astype(BF16)
            total = total + dot(ones, grad_pre, 1, 0)
            outer = outer + dot(hidden_low[rows, :], grad_pre, 0, 0)
            part = dot(grad_pre, expand, 1, 1)

            @pl.when(step == half_steps)
            def _():
                resid_out[rows, :] = resid_ref[rows, :] + part

            @pl.when(step > half_steps)
            def _():
                resid_out[rows, :] += part

        d_w1[0] = outer.astype(BF16).reshape(d_w1.shape[1:])
        vec_sums[pl.ds(step - half_steps, 1), :] = total[0:1, :]

    @pl.when(step == half_steps)
    def _():
        for job in jobs:
            job.core_stage()

    @pl.when(step == half_steps + 1)
    def _():
        jobs[0].one_stage()
        jobs[1].one_stage()

    @pl.when(step == half_steps + 2)
    def _():
        jobs[2].one_stage()
        jobs[3].one_stage()
        jobs[0].two_stage()

    @pl.when(step == pl.num_programs(0) - 1)
    def _():
        for job in jobs[1:]:
            job.two_stage()
        jobs[0].z_hop(1)
        merge = wo_ref[...].reshape(feats, feats)
        sums = [jnp.zeros((1, feats), F32)] * 3
        outer = jnp.zeros((feats, feats), F32)
        for rows in blocks:
            grad_hidden = resid_out[rows, :]
            normed = normed_ref[rows, :]
            grad = normalize_back(normed, inv_ref[rows, 0:1], vec(G1) * grad_hidden)
            resid_out[rows, :] = grad
            low = grad.astype(BF16)
            grad_ctx[rows, :] = dot(low, merge, 1, 1).astype(BF16)
            outer = outer + dot(ctx_ref[rows, :], low, 0, 0)
            terms = (grad_hidden * normed, grad_hidden, low.astype(F32))
            sums = [
                total + jnp.sum(term, axis=0, keepdims=True) for total, term in zip(sums, terms)
            ]
        d_wo[...] = outer.astype(BF16).reshape(d_wo.shape)
        jobs[1].z_hop(1)
        jobs[0].z_hop(2)
        row = lax.broadcasted_iota(jnp.int32, (16, 1), 0)
        lines = sums + [vec_in[k : k + 1, :] for k in range(3)]
        lines = lines + [vec_sums[k : k + 1, :] for k in range(4)]
        packed = jnp.zeros((16, feats), F32)
        for k, line in enumerate(lines):
            packed = jnp.where(row == k, line, packed)
        vec_out[...] = packed.astype(BF16)

        tail = [functools.partial(Reduce.z_hop, hop=hop) for hop in range(1, seq_size)]
        tail.append(Reduce.finish)
        plan = [(job, max(0, k - 1), tail[max(0, 2 - k) :]) for k, job in enumerate(jobs)]
        for time in range(max(wait + len(stages) for _, wait, stages in plan)):
            for job, wait, stages in plan:
                if 0 <= time - wait < len(stages):
                    stages[time - wait](job)
        for job in jobs:
            job.drain()
        outs.finish()


def feed_back(
    seq_size, seq_count, act, slope, w1_full, w2_full, resid, normed, inv, ctx, wo_full, vecs,
    vec_in, out_rows,
):
    seq_len, feats = ctx.shape
    shard, w2_rows = w1_full.shape[1], w2_full.shape[1]
    steps = act.shape[1] // feats
    blk = seq_len // seq_size
    once = pl.Buffered(1)
    any_spec = pl.BlockSpec(memory_space=pl.ANY)
    dma = pltpu.SemaphoreType.DMA

    def whole(shape, mode=None):
        return pl.BlockSpec(shape, lambda j: (0,) * len(shape), pipeline_mode=mode)

    def first(j):
        return jnp.minimum(j, steps - 1)

    def second(j):
        return jnp.maximum(j - steps, 0)

    rows = (seq_len, feats)
    return pl.pallas_call(
        functools.partial(feed_back_kernel, seq_size, seq_count, min(256, seq_len)),
        grid=(2 * steps,),
        in_specs=[
            pl.BlockSpec(rows, lambda j: (0, first(j))),
            pl.BlockSpec(rows, lambda j: (0, second(j))),
            pl.BlockSpec((8, shard, feats), lambda j: (0, 0, second(j))),
            pl.BlockSpec((8 // steps, w2_rows, feats), lambda j: (second(j), 0, 0)),
            whole(rows, once), whole(rows, once), whole(inv.shape, once), whole(rows, once),
            whole(wo_full.shape, once), whole(vecs.shape, once), whole(vec_in.shape, once),
            any_spec,
        ],
        out_specs=[
            pl.BlockSpec((1, 8, shard, feats), lambda j: (second(j), 0, 0, 0)),
            whole(rows), whole(rows), whole(wo_full.shape), whole((16, feats)),
            any_spec, any_spec,
        ],
        out_shape=[
            jax.ShapeDtypeStruct((steps, 8, shard, feats), BF16),
            jax.ShapeDtypeStruct(rows, F32), jax.ShapeDtypeStruct(rows, BF16),
            jax.ShapeDtypeStruct(wo_full.shape, BF16), jax.ShapeDtypeStruct((16, feats), BF16),
            jax.ShapeDtypeStruct((w2_rows, feats), BF16),
            jax.ShapeDtypeStruct((seq_count, blk, feats), BF16),
        ],
        scratch_shapes=[
            pltpu.VMEM(rows, BF16), pltpu.VMEM(rows, BF16), pltpu.VMEM((8, w2_rows, feats), BF16),
            pltpu.VMEM((8, feats), F32),
        ]
        + Reduce.scratch(4, w2_rows // 4, feats)
        + Reduce.semaphores(4)
        + [dma((seq_size,)), dma((seq_count,)), dma((1,))],
        compiler_params=pltpu.CompilerParams(
            collective_id=4, has_side_effects=True, vmem_limit_bytes=VMEM_MAX
        ),
    )(
        act, slope, w1_full, w2_full, resid, normed, inv, ctx, wo_full, vecs, vec_in, out_rows
    )


def backward_kernel(seq_size, seq_count, rows_blk, *refs):
    refs = list(refs)

    def take(count):
        got = refs[:count]
        del refs[:count]
        return got

    q_ref, k_ref, v_ref, ctx_ref, grad_ref, probs_ref, vec_ref = take(7)
    x_in, qkv_in, resid_in, d_w1, d_wo = take(5)
    w1_total, wo_total, wq_total, wk_total, wv_total, vec_total, token_out = take(7)
    key_acc, value_acc, grads_all, x_rows, qkv_mat, resid, token_rows = take(7)
    mats = take(3)
    (vec_src,) = take(1)
    w1_count = d_w1.shape[0]
    mat_count = w1_count + 4
    bufs = take(6)
    vec_bufs = take(6)
    sems = take(9)
    (load_sem,) = take(1)
    token_sems = take(3)

    step = pl.program_id(0)
    place = Place(seq_size, seq_count)
    seq_len, feats = x_rows.shape

    def outer_source(c):
        if c < w1_count:
            return lambda shard: d_w1.at[c, shard]
        if c == w1_count:
            return lambda shard: d_wo.at[shard]
        return lambda shard: mats[c - w1_count - 1].at[shard]

    outer_totals = [w1_total.at[:, pl.ds(c * feats, feats)] for c in range(w1_count)]
    outer_totals += [wo_total, wq_total, wk_total, wv_total]
    jobs = [
        Reduce(place, outer_source(c), outer_totals[c], [buf.at[c] for buf in bufs], sems, c)
        for c in range(mat_count)
    ]
    jobs.append(
        Reduce(
            place, lambda shard: vec_src.at[shard], vec_total, [buf.at[0] for buf in vec_bufs],
            sems, mat_count,
        )
    )
    ready = w1_count + 1
    blk = seq_len // seq_size
    loads = [
        pltpu.make_async_copy(src, dst, load_sem.at[k])
        for k, (src, dst) in enumerate(((x_in, x_rows), (qkv_in, qkv_mat), (resid_in, resid)))
    ]
    tokens = RowsOut(place, token_rows, token_out, token_sems)

    @pl.when(step == 0)
    def _():
        place.barrier()
        for job in jobs[:ready]:
            job.begin()
        for load in loads:
            load.start()
        jobs[0].core_stage()

    column = pl.multiple_of(step * LANES, LANES)

    def store(which, rows, values):
        grads_all[which, rows, pl.ds(column, LANES)] = values

    attend_back_pair(
        q_ref, k_ref, v_ref, ctx_ref, grad_ref, probs_ref, store, key_acc, value_acc, rows_blk
    )

    core, one, two = Reduce.core_stage, Reduce.one_stage, Reduce.two_stage
    hops = [functools.partial(Reduce.z_hop, hop=hop) for hop in range(1, seq_size)]
    tail = hops + [Reduce.finish]
    ticks = (
        ((core, 1), (core, 2)),
        ((one, 0), (core, 3), (core, 4)),
        ((one, 1), (one, 2)),
        ((two, 0), (one, 3)),
        ((two, 1), (two, 2), (one, 4), (hops[0], 0)),
    )
    for at_step, stages in enumerate(ticks):

        @pl.when(step == at_step)
        def _():
            for stage, chunk in stages:
                stage(jobs[chunk])

    @pl.when(step == pl.num_programs(0) - 1)
    def _():
        for load in loads:
            load.wait()
        for chunk in (3, 4):
            two(jobs[chunk])
        hops[0](jobs[1])
        hops[0](jobs[2])
        hops[1](jobs[0])
        after = (
            ((hops[0], 3), (hops[1], 1), (hops[2], 0)),
            ((hops[0], 4), (hops[1], 2), (hops[2], 1), (Reduce.finish, 0)),
            ((hops[1], 3), (hops[2], 2), (Reduce.finish, 1)),
            ((hops[1], 4), (hops[2], 3), (Reduce.finish, 2)),
        )
        for pos in range(seq_size):
            rows = pl.ds(pos * blk, blk)
            part = resid[rows, :]
            for which in range(3):
                mat = qkv_mat[:, :, which * feats : (which + 1) * feats].reshape(feats, feats)
                part = part + dot(grads_all[which, rows, :], mat, 1, 1)
            token_rows[rows, :] = part.astype(BF16)
            tokens.start(pos)
            for stage, chunk in after[pos]:
                stage(jobs[chunk])
        for which in range(3):
            outer_sum = dot(x_rows[...], grads_all[which], 0, 0).astype(BF16)
            mats[which][...] = outer_sum.reshape(mats[which].shape)
            jobs[ready + which].begin()
            if which:
                core(jobs[ready + which - 1])
        ones = jnp.ones((16, seq_len), BF16)
        grad_bq = dot(ones, grads_all[0], 1, 0)
        grad_bv = dot(ones, grads_all[2], 1, 0)
        row = lax.broadcasted_iota(jnp.int32, (16, 1), 0)
        biases = jnp.where(row == 0, grad_bq, grad_bv).astype(BF16)
        for shard in range(8):
            vec_src[shard, 0:16, :] = vec_ref[...]
            vec_src[shard, 16:32, :] = biases
        jobs[-1].begin()
        core(jobs[-2])
        core(jobs[-1])

        plan = [(jobs[3], 0, [Reduce.finish]), (jobs[4], 0, tail[2:])]
        for k, job in enumerate(jobs[ready:]):
            plan.append((job, k, [one, two] + tail))
        for time in range(max(wait + len(stages) for _, wait, stages in plan)):
            for job, wait, stages in plan:
                if 0 <= time - wait < len(stages):
                    stages[time - wait](job)
        for job in jobs:
            job.drain()
        tokens.finish()


def backward_all(
    seq_size, seq_count, query, key, value, ctx, grad_ctx, probs, vecs, inputs, qkv_full, resid,
    d_w1, d_wo,
):
    seq_len, feats = ctx.shape
    blk = seq_len // seq_size
    shard = qkv_full.shape[1]
    w1_count = d_w1.shape[0]
    count = w1_count + 4
    any_spec = pl.BlockSpec(memory_space=pl.ANY)
    cols = pl.BlockSpec((seq_len, LANES), lambda g: (0, g))
    dma = pltpu.SemaphoreType.DMA
    mat = jax.ShapeDtypeStruct((shard, feats), BF16)
    return pl.pallas_call(
        functools.partial(backward_kernel, seq_size, seq_count, min(512, seq_len)),
        grid=(feats // LANES,),
        in_specs=[cols] * 5
        + [
            pl.BlockSpec((2, seq_len, seq_len), lambda g: (g, 0, 0)),
            pl.BlockSpec(vecs.shape, lambda g: (0, 0)),
        ]
        + [any_spec] * 5,
        out_specs=[any_spec] * 7,
        out_shape=[jax.ShapeDtypeStruct((shard, w1_count * feats), BF16), mat, mat, mat, mat]
        + [
            jax.ShapeDtypeStruct((32, feats), BF16),
            jax.ShapeDtypeStruct((seq_count, blk, feats), BF16),
        ],
        scratch_shapes=[pltpu.VMEM((2, HEAD, seq_len), F32)] * 2
        + [
            pltpu.VMEM((3, seq_len, feats), BF16),
            pltpu.VMEM((seq_len, feats), BF16),
            pltpu.VMEM(qkv_full.shape, BF16),
            pltpu.VMEM((seq_len, feats), F32),
            pltpu.VMEM((seq_len, feats), BF16),
        ]
        + [pltpu.VMEM((8, shard, feats), BF16)] * 3
        + [pltpu.VMEM((8, 32, feats), BF16)]
        + Reduce.scratch(count, shard, feats)
        + Reduce.scratch(1, 32, feats)
        + Reduce.semaphores(count + 1)
        + [dma((3,)), dma((seq_size,)), dma((seq_count,)), dma((1,))],
        compiler_params=pltpu.CompilerParams(
            collective_id=1, has_side_effects=True, vmem_limit_bytes=VMEM_MAX
        ),
    )(query, key, value, ctx, grad_ctx, probs, vecs, inputs, qkv_full, resid, d_w1, d_wo)


def widen_kernel(*refs):
    count = len(refs) // 2
    for source, dest in zip(refs[:count], refs[count:]):
        dest[...] = source[...].astype(F32)


def widen(arrays):
    return pl.pallas_call(
        widen_kernel,
        out_shape=[jax.ShapeDtypeStruct(item.shape, F32) for item in arrays],
        compiler_params=pltpu.CompilerParams(vmem_limit_bytes=VMEM_LIMIT),
    )(*arrays)


def column_sum(rows):
    return jnp.sum(rows, axis=0, dtype=F32)


def per_device(mesh_shape, tokens, lengths, *rest):
    weights, upstream = rest[:15], rest[15]
    dp_size, seq_size = mesh_shape
    seq_count, row_count, feats = tokens.shape
    dp_index = lax.axis_index("dp")
    here = lax.axis_index("seq")
    spare = seq_size - seq_count

    def owner_shift(dp):
        return spare * (dp % 2)

    my_seq = jnp.clip(here - owner_shift(dp_index), 0, seq_count - 1)

    def owned_by(dp, pos):
        seq = pos - owner_shift(dp)
        return 0 <= seq < seq_count

    def shift_pairs(step, to_owner):
        pairs = []
        for dp in range(dp_size):
            for pos in range(seq_size):
                dest = (pos + step) % seq_size
                if owned_by(dp, dest if to_owner else pos):
                    pairs.append((dp * seq_size + pos, dp * seq_size + dest))
        return pairs

    def gather(piece):
        return lax.all_gather(piece, "dp", axis=0, tiled=True)

    def to_owners(blocks):
        pieces = []
        for step in range(seq_size):
            dest = (here + step) % seq_size
            seq = jnp.clip(dest - owner_shift(dp_index), 0, seq_count - 1)
            piece = lax.dynamic_index_in_dim(blocks, seq, 0, keepdims=False)
            if step == 0:
                owner = (here >= owner_shift(dp_index)) & (here < owner_shift(dp_index) + seq_count)
                piece = jnp.where(owner, piece, jnp.zeros_like(piece))
            else:
                piece = lax.ppermute(piece, ("dp", "seq"), shift_pairs(step, True))
            pieces.append(piece)
        order = (here - jnp.arange(seq_size)) % seq_size
        return jnp.take(jnp.stack(pieces), order, axis=0).reshape(-1, feats)

    def from_owners(rows):
        pieces = rows.reshape(seq_size, row_count, feats)
        arrived = []
        for step in range(seq_size):
            piece = lax.dynamic_index_in_dim(pieces, (here - step) % seq_size, 0, keepdims=False)
            if step:
                piece = lax.ppermute(piece, ("dp", "seq"), shift_pairs(seq_size - step, False))
            arrived.append(piece)
        stack = jnp.stack(arrived)
        order = (jnp.arange(seq_count) + owner_shift(dp_index) - here) % seq_size
        return jnp.take(stack, order, axis=0)

    wq, bq, wk, wv, bv, wo, bo, g1, b1, w1, c1, w2, c2, g2, b2 = weights
    shard_rows = feats // dp_size
    direct = dp_size == 8 and shard_rows % 32 == 0
    vec_parts = (bq, bv, bo, g1, b1, c2, g2, b2, c1)
    vec_sizes = [item.shape[0] for item in vec_parts]
    vec_len = sum(vec_sizes)
    vec_rows = -(-vec_len // (32 * LANES)) * 32
    packed = jnp.concatenate(vec_parts).astype(BF16)
    seq_len = seq_size * row_count
    position = lax.iota(jnp.int32, seq_len)
    valid_len = lax.dynamic_index_in_dim(lengths, my_seq, 0, keepdims=False)
    key_bias = jnp.where(position < valid_len, 0.0, 8.0 * NEG_FILL).astype(F32).reshape(1, seq_len)

    if direct:
        packed = jnp.pad(packed, (0, vec_rows * LANES - vec_len)).reshape(vec_rows, LANES)
        inputs, qkv_full, packed, w2_part, w1_part, wo_part = start_all(
            seq_size, tokens, (wq, wk, wv), packed, w2, w1, wo
        )
        packed = packed.reshape(dp_size, vec_rows * LANES)
        qkv_mat = qkv_full.reshape(feats, 3 * feats)
    else:
        qkv_mat = gather(jnp.concatenate([wq, wk, wv], axis=1).astype(BF16))
        packed = lax.all_gather(packed, "dp", axis=0, tiled=False)
        merge_mat, expand_mat, reduce_mat = [gather(item.astype(BF16)) for item in (wo, w1, w2)]
    vecs = []
    start = 0
    for size in vec_sizes:
        vecs.append(packed[:, start : start + size].reshape(1, -1).astype(F32))
        start += size
    bq, bv, bo, g1, b1, c2, g2, b2, c1 = vecs

    if direct:
        query, key, value, ctx, probs, dy, w2_full, w1_full, wo_full = forward_all(
            seq_size, key_bias, inputs, qkv_full, bq, bv, upstream, w2_part, w1_part, wo_part
        )
        vec_rows = jnp.concatenate([item.reshape(-1, feats) for item in vecs])
        vec_rows = jnp.pad(vec_rows, ((0, 16 - vec_rows.shape[0]), (0, 0)))
        act, slope, out_rows, grad_resid2, normed1, inv1, second_sums = feed_forward(
            ctx, inputs, wo_full, vec_rows, w1_full, w2_full, dy
        )
        d_w1, grad_resid1, grad_ctx, d_wo, vec_sums, sum_w2, output = feed_back(
            seq_size, seq_count, act, slope, w1_full, w2_full, grad_resid2, normed1, inv1, ctx,
            wo_full, vec_rows, second_sums, out_rows,
        )
        *sums, vec_sum, token_grad = backward_all(
            seq_size, seq_count, query, key, value, ctx, grad_ctx, probs, vec_sums, inputs,
            qkv_full, grad_resid1, d_w1, d_wo,
        )
        sum_w2, sum_w1, s_wo, s_wq, s_wk, s_wv, vec_sum = widen([sum_w2] + sums + [vec_sum])

        def own_part(first, length):
            rows = vec_sum[first : first + -(-length * dp_size // feats)].reshape(-1)
            return lax.dynamic_slice(rows, (dp_index * length,), (length,))

        s_g1, s_b1, s_bo, s_g2, s_b2, s_c2 = [own_part(k, shard_rows) for k in range(6)]
        s_c1 = own_part(6, c1.shape[1] // dp_size)
        s_bq, s_bv = own_part(16, shard_rows), own_part(17, shard_rows)
    else:
        inputs = to_owners(tokens)
        dy = to_owners(upstream).astype(F32)
        qkv = dot(inputs, qkv_mat, 1, 0)
        query = (qkv[:, :feats] + bq).astype(BF16)
        key = qkv[:, feats : 2 * feats].astype(BF16)
        value = (qkv[:, 2 * feats :] + bv).astype(BF16)
        ctx, probs = attend(key_bias, query, key, value)
        normed1, inv1 = normalize(inputs.astype(F32) + dot(ctx, merge_mat, 1, 0) + bo)
        hidden = normed1 * g1 + b1
        hidden_low = hidden.astype(BF16)
        pre = dot(hidden_low, expand_mat, 1, 0) + c1
        phi_cum = 0.5 * (1.0 + lax.erf(pre * INV_SQRT2))
        act = (pre * phi_cum).astype(BF16)
        slope = (phi_cum + pre * (INV_SQRT_2PI * jnp.exp(-0.5 * pre * pre))).astype(BF16)
        normed2, inv2 = normalize(hidden + dot(act, reduce_mat, 1, 0) + c2)
        result = (normed2 * g2 + b2).astype(BF16)
        output = from_owners(result)

        d_g2 = column_sum(dy * normed2)
        d_b2 = column_sum(dy)
        grad_resid2 = normalize_back(normed2, inv2, g2 * dy)
        grad_ffn = grad_resid2.astype(BF16)
        d_w2 = dot(act, grad_ffn, 0, 0).astype(BF16)
        d_c2 = column_sum(grad_ffn)
        grad_pre = (dot(grad_ffn, reduce_mat, 1, 1) * slope.astype(F32)).astype(BF16)
        d_w1 = dot(hidden_low, grad_pre, 0, 0).astype(BF16)
        d_c1 = column_sum(grad_pre)
        grad_hidden = grad_resid2 + dot(grad_pre, expand_mat, 1, 1)
        d_g1 = column_sum(grad_hidden * normed1)
        d_b1 = column_sum(grad_hidden)
        grad_resid1 = normalize_back(normed1, inv1, g1 * grad_hidden)
        grad_att = grad_resid1.astype(BF16)
        d_wo = dot(ctx, grad_att, 0, 0).astype(BF16)
        d_bo = column_sum(grad_att)
        grad_ctx = dot(grad_att, merge_mat, 1, 1).astype(BF16)
        grad_qkv = attend_back(query, key, value, ctx, grad_ctx, probs)
        token_rows = grad_resid1
        d_qkv = []
        for which in range(3):
            mat = qkv_mat[:, which * feats : (which + 1) * feats]
            token_rows = token_rows + dot(grad_qkv[which], mat, 1, 1)
            d_qkv.append(dot(inputs, grad_qkv[which], 0, 0).astype(BF16))
        d_bq = column_sum(grad_qkv[0])
        d_bv = column_sum(grad_qkv[2])
        token_grad = from_owners(token_rows.astype(BF16))
        vec_grads = (d_bq, d_bv, d_bo, d_g1, d_b1, d_c2, d_g2, d_b2, d_c1)
        vec_pack = jnp.concatenate([item.reshape(dp_size, -1) for item in vec_grads], axis=1)
        vec_cols = -(-vec_len // (shard_rows * LANES)) * LANES
        vec_pack = jnp.pad(vec_pack, ((0, 0), (0, shard_rows * vec_cols - vec_len)))
        vec_pack = vec_pack.reshape(feats, vec_cols).astype(BF16)

        def reduce(full):
            own = lax.psum_scatter(full, "dp", scatter_dimension=0, tiled=True)
            return lax.psum(own, "seq").astype(F32)

        sum_w2 = reduce(d_w2)
        sum_w1 = reduce(d_w1)
        sum_rest = reduce(jnp.concatenate([d_wo] + d_qkv + [vec_pack], axis=1))
        s_wo, s_wq, s_wk, s_wv = [sum_rest[:, i * feats : (i + 1) * feats] for i in range(4)]
        flat = sum_rest[:, 4 * feats :].reshape(-1)
        out_vecs = []
        start = 0
        for size in vec_sizes:
            out_vecs.append(flat[start : start + size])
            start += size
        s_bq, s_bv, s_bo, s_g1, s_b1, s_c2, s_g2, s_b2, s_c1 = out_vecs
    return (
        output,
        token_grad,
        s_wq,
        s_bq,
        s_wk,
        s_wv,
        s_bv,
        s_wo,
        s_bo,
        s_g1,
        s_b1,
        sum_w1,
        s_c1,
        sum_w2,
        s_c2,
        s_g2,
        s_b2,
    )


def solution(mesh):
    rows, mat, vec = P("dp", "seq", None), P("dp", None), P("dp")
    params = (mat, vec, mat, mat, vec, mat, vec, vec, vec, mat, vec, mat, vec, vec, vec)
    return jax.shard_map(
        functools.partial(per_device, (mesh.shape["dp"], mesh.shape["seq"])),
        mesh=mesh,
        in_specs=(rows, vec) + params + (rows,),
        out_specs=(rows, rows) + params,
        check_vma=False,
    )
```

profile of v0, /device:TPU:0, one launch (start us, length us, event | category | flops | bytes accessed | tf_op | source)
XLA Modules:
  0.0 329.2 jit_solution(16620618367599589208)
XLA Ops:
  0.7 1.2 dynamic_slice.47
  1.9 1.2 compare_select_fusion.bias_ref
  3.2 0.7 convert.44
  3.8 0.7 convert.36
  4.5 0.7 convert.37
  5.2 0.7 convert.38
  5.8 0.7 convert.39
  6.5 0.7 convert.40
  7.1 0.7 convert.41
  7.8 0.7 convert.42
  8.4 0.7 convert.43
  9.1 0.1 concatenate.7
  9.2 0.6 pad_bitcast_fusion.vecs
  9.8 39.1 %shard_map.305 = (bf16[1024,768]{1,0:T(8,128)(2,1)}, bf16[8,96,2304]{2,1,0:T(8,128)(2,1)}, bf16[8,32,128]{2,1,0:T(8,128)(2,1)}, bf16[8,384,768]{2,1,0:T(8,128)(2...) custom-call(bf16[3,256,768]{2,1,0:T(8,128)(2,1)} %tokens.1, f32[96,768]{1,0:T(8,128)} %wq.1, ...), custom_call_target="tpu_custom_call" | custom-call | tf_op jit(solution)/shard_map/pallas_call | solution.py:356
  48.9 0.9 copy.40
  49.8 0.1 slice_convert_fusion.1
  49.9 0.7 reshape.201.bq_ref
  50.5 0.7 reshape.202.bv_ref
  51.2 0.0 copy-start.2
  51.2 0.0 copy-start.3
  51.2 41.7 %shard_map.306 = (bf16[1024,768]{1,0:T(8,128)(2,1)}, bf16[1024,768]{1,0:T(8,128)(2,1)}, bf16[1024,768]{1,0:T(8,128)(2,1)}, bf16[1024,768]{1,0:T(8,128)(2,1)}, bf...) custom-call(f32[1,1024]{1,0:T(1,128)} %compare_select_fusion.bias_re, ...), custom_call_target="tpu_custom_call", output_to_operand_aliasing={{6}: (8, {}), {7}: (9, {}), {8}: (10, {})} | custom-call | tf_op jit(solution)/shard_map/pallas_call | solution.py:445
  92.9 0.1 reshape.203
  93.0 0.1 reshape.204
  93.1 0.1 reshape.205
  93.2 0.1 reshape.206
  93.2 0.1 reshape.207
  93.3 0.1 reshape.208
  93.4 0.0 copy-done.2
  93.4 0.0 copy-done.3
  93.4 0.1 concatenate.8
  93.5 0.6 pad.9.vec_ref.refs_9_
  94.1 30.3 %shard_map.307 = (bf16[1024,3072]{1,0:T(8,128)(2,1)}, bf16[1024,3072]{1,0:T(8,128)(2,1)}, bf16[1024,768]{1,0:T(8,128)(2,1)}, f32[1024,768]{1,0:T(8,128)}, f32[10...) custom-call(bf16[1024,768]{1,0:T(8,128)(2,1)} %get-tuple-element.66.ctx_ref.refs_7_.refs_3_, ...), custom_call_target="tpu_custom_call" | custom-call | tf_op jit(solution)/shard_map/pallas_call | solution.py:800
  124.5 75.4 %shard_map.308 = (bf16[4,8,96,768]{3,2,1,0:T(8,128)(2,1)}, f32[1024,768]{1,0:T(8,128)}, bf16[1024,768]{1,0:T(8,128)(2,1)}, bf16[8,96,768]{2,1,0:T(8,128)(2,1)}, ...) custom-call(bf16[1024,3072]{1,0:T(8,128)(2,1)} %get-tuple-element.71.refs_0_, ...), custom_call_target="tpu_custom_call" | custom-call | tf_op jit(solution)/shard_map/pallas_call | solution.py:983
  199.8 118.6 %shard_map.309 = (bf16[96,3072]{1,0:T(8,128)(2,1)}, bf16[96,768]{1,0:T(8,128)(2,1)}, bf16[96,768]{1,0:T(8,128)(2,1)}, bf16[96,768]{1,0:T(8,128)(2,1)}, bf16[96,7...) custom-call(bf16[1024,768]{1,0:T(8,128)(2,1)} %get-tuple-element.79.refs_0_, ...), custom_call_target="tpu_custom_call" | custom-call | tf_op jit(solution)/shard_map/pallas_call | solution.py:1178
  318.4 0.0 copy-start
  318.5 3.4 %shard_map.310 = (f32[384,768]{1,0:T(8,128)}, f32[96,3072]{1,0:T(8,128)}, f32[96,768]{1,0:T(8,128)}, f32[96,768]{1,0:T(8,128)}, f32[96,768]{1,0:T(8,128)}, /*index=5*/f32[96,768]{1,0:T(8,128)}, f32[32,768]{1,0:T(8,128)}) custom-call(bf16[384,768]{1,0:T(8,128)(2,1)} %get-tuple-element.89.refs_0_, bf16[96,3072]{1,0:T(8,128)(2,1)} %get-tuple-element.90.refs_1_, ...), custom_call_target="tpu_custom_call" | custom-call | tf_op jit(solution)/shard_map/pallas_call | solution.py:1220
  321.8 0.0 copy-start.1
  321.8 1.0 fusion.8
  322.9 0.6 fusion.6
  323.5 0.8 slice.68
  324.3 0.7 dynamic_slice.58
  324.9 0.6 fusion.4
  325.5 0.6 fusion.2
  326.1 0.6 fusion
  326.7 0.0 copy-done
  326.7 1.0 copy.46
  327.7 0.0 copy-done.1
  327.7 1.0 copy.47
  (3 shorter events, 0.0 us)
Async XLA Ops:
  51.2 42.2 %copy-start.2 = (f32[1,768]{1,0:T(1,128)S(1)}, f32[1,768]{1,0:T(1,128)}, u32[]{:S(2)}) copy-start(f32[1,768]{1,0:T(1,128)} %reshape.201.bq_ref) | copy-start | bytes 9220
  51.2 42.2 %copy-start.3 = (f32[1,768]{1,0:T(1,128)S(1)}, f32[1,768]{1,0:T(1,128)}, u32[]{:S(2)}) copy-start(f32[1,768]{1,0:T(1,128)} %reshape.202.bv_ref) | copy-start | bytes 9220
  318.4 8.2 %copy-start = (bf16[3,256,768]{2,1,0:T(8,128)(2,1)S(1)}, bf16[3,256,768]{2,1,0:T(8,128)(2,1)}, u32[]{:S(2)}) copy-start(bf16[3,256,768]{2,1,0:T(8,128)(2,1)} %get-tuple-element.144) | copy-start | bytes 3538948
  321.8 5.9 %copy-start.1 = (bf16[3,256,768]{2,1,0:T(8,128)(2,1)S(1)}, bf16[3,256,768]{2,1,0:T(8,128)(2,1)}, u32[]{:S(2)}) copy-start(bf16[3,256,768]{2,1,0:T(8,128)(2,1)} %get-tuple-element.145) | copy-start | bytes 3538948
where the time goes:
time: 335 us; the launch traced here: 329 us
  Pallas kernels  309 us (92%)
  local copies, waits for them, and re-layouts  12.2 us (4%)
  other arithmetic  7.26 us (2%)
    pallas_call x1, Pallas kernels, backward_all(): pl.pallas_call(functools.partial(backward_kernel, seq_size, seq_count, mi...  119 us
    pallas_call x1, Pallas kernels, feed_back(): pl.pallas_call(functools.partial(feed_back_kernel, seq_size, seq_count, m...  75.4 us
    pallas_call x1, Pallas kernels, forward_all(): pl.pallas_call(functools.partial(forward_kernel, seq_size, seq_count, min...  41.7 us
    pallas_call x1, Pallas kernels, start_all(): pl.pallas_call(functools.partial(start_kernel, seq_size, seq_count), in_s...  39.1 us
    pallas_call x1, Pallas kernels, feed_forward(): pl.pallas_call(functools.partial(feed_kernel, min(256, seq_len)), grid=(s...  30.3 us

commit v1 on v0

--- a/solution.py
+++ b/solution.py
@@ -62,7 +62,8 @@
 
 
 def attend_back_pair(
-    q_ref, k_ref, v_ref, ctx_ref, grad_ref, probs_ref, store, key_acc, value_acc, rows_blk
+    q_ref, k_ref, v_ref, ctx_ref, grad_ref, probs_ref, store, key_acc, value_acc, rows_blk,
+    between=None,
 ):
     seq_len = q_ref.shape[0]
     lane = lax.broadcasted_iota(jnp.int32, (1, LANES), 1)
@@ -93,6 +94,8 @@
                 value_acc[head] += grad_value
         mixed = jnp.where(lane < HEAD, grad_query[0], grad_query[1])
         store(0, rows, (0.125 * mixed).astype(BF16))
+        if between is not None:
+            between(blk)
     everything = pl.ds(0, seq_len)
     grad_key = jnp.concatenate([key_acc[0], key_acc[1]], axis=0)
     store(1, everything, (0.125 * grad_key).T.astype(BF16))
@@ -283,11 +286,12 @@
 
 
 def start_kernel(
-    seq_size, seq_count, tokens, wq, wk, wv, vecs, w2, w1, wo,
-    rows_out, qkv_full, vec_full, w2_full, w1_full, wo_full,
-    qkv_low, w2_low, w1_low, wo_low, row_buf,
-    row_send, row_recv, row_local, sem_a, sem_b, sem_c, sem_d, own_sem,
+    seq_size, seq_count, tokens, wq, wk, wv, w2, w1, wo, *refs,
 ):
+    vec_refs, refs = refs[:9], refs[9:]
+    rows_out, qkv_full, vec_full, w2_full, w1_full, wo_full = refs[:6]
+    qkv_low, w2_low, w1_low, wo_low, row_buf, vec_wide, vecs = refs[6:13]
+    row_send, row_recv, row_local, sem_a, sem_b, sem_c, sem_d, own_sem = refs[13:]
     place = Place(seq_size, seq_count)
     sems = (sem_a, sem_b, sem_c, sem_d)
     rows = RowsIn(place, tokens, rows_out, row_buf, (row_send, row_recv, row_local))
@@ -303,6 +307,12 @@
     place.barrier()
     rows.start()
     feats = wq.shape[1]
+    vec_wide[...] = jnp.zeros_like(vec_wide)
+    for k, item in enumerate(vec_refs[:8]):
+        vec_wide[k : k + 1, 0 : item.shape[1]] = item[...]
+    for k in range(vec_refs[8].shape[1] // LANES):
+        vec_wide[8 + k : 9 + k, :] = vec_refs[8][:, k * LANES : (k + 1) * LANES]
+    vecs[...] = vec_wide[...].astype(BF16)
     for k, item in enumerate((wq, wk, wv)):
         qkv_low[:, k * feats : (k + 1) * feats] = item[...].astype(BF16)
     for item in first:
@@ -355,30 +365,54 @@
 
     return pl.pallas_call(
         functools.partial(start_kernel, seq_size, seq_count),
-        in_specs=[any_spec] + [vmem_spec] * 7,
+        in_specs=[any_spec] + [vmem_spec] * (6 + len(vecs)),
         out_specs=[any_spec] * 6,
         out_shape=[
             jax.ShapeDtypeStruct((seq_size * blk, feats), BF16),
-            full(shard, 3 * feats), full(*vecs.shape), full(*w2.shape), full(*w1.shape),
+            full(shard, 3 * feats), full(32, LANES), full(*w2.shape), full(*w1.shape),
             full(*wo.shape),
         ],
         scratch_shapes=[
             pltpu.VMEM((shard, 3 * feats), BF16), pltpu.VMEM(w2.shape, BF16),
             pltpu.VMEM(w1.shape, BF16), pltpu.VMEM(wo.shape, BF16), pltpu.VMEM((blk, feats), BF16),
+            pltpu.VMEM((32, LANES), F32), pltpu.VMEM((32, LANES), BF16),
             dma((seq_count,)), dma((seq_size,)), dma((seq_size,)),
             dma((5, 6)), dma((5, 6)), dma((5, 7)), dma((5, 7)), dma((5,)),
         ],
         compiler_params=pltpu.CompilerParams(
             collective_id=2, has_side_effects=True, vmem_limit_bytes=VMEM_LIMIT
         ),
-    )(tokens, *qkv_parts, vecs, w2, w1, wo)
+    )(tokens, *qkv_parts, w2, w1, wo, *vecs)
+
+
+BQ, BV, BO, G1, B1, C2, G2, B2, C1 = range(9)
+
+
+def unpack_vectors(full, out):
+    shards, _, _ = full.shape
+    feats = out.shape[1]
+    part = feats // shards
+    lane = lax.broadcasted_iota(jnp.int32, (LANES, feats), 0)
+    column = lax.broadcasted_iota(jnp.int32, (LANES, feats), 1)
+    rows = jnp.zeros((16, feats), F32)
+    for k in range(shards):
+        place = ((lane < part) & (column == lane + k * part)).astype(BF16)
+        rows = rows + dot(full[k, 0:16, :], place, 1, 0)
+    out[...] = rows
+    long = feats * 4 // shards
+    for k in range(shards):
+        row, start = C1 + k * long // feats, k * long % feats
+        for j in range(long // LANES):
+            out[row : row + 1, start + j * LANES : start + (j + 1) * LANES] = full[
+                k, 8 + j : 9 + j, :
+            ].astype(F32)
 
 
 def forward_kernel(
     seq_size, seq_count, rows_blk,
-    bias_ref, x_ref, wq_ref, wk_ref, wv_ref, bq_ref, bv_ref, upstream, w2_in, w1_in, wo_in,
-    q_ref, k_ref, v_ref, ctx_ref, probs_ref, dy_out, w2_full, w1_full, wo_full,
-    row_buf, row_send, row_recv, row_local, sem_a, sem_b, sem_c, sem_d,
+    len_ref, x_ref, wq_ref, wk_ref, wv_ref, vec_full, upstream, w2_in, w1_in, wo_in,
+    q_ref, k_ref, v_ref, ctx_ref, probs_ref, vec_out, dy_out, w2_full, w1_full, wo_full,
+    bias_ref, row_buf, row_send, row_recv, row_local, sem_a, sem_b, sem_c, sem_d,
 ):
     step = pl.program_id(0)
     last = pl.num_programs(0) - 1
@@ -401,14 +435,19 @@
         for item in later:
             item.to_core(6, 0, 1)
         rows.own(seq_size)
+        unpack_vectors(vec_full, vec_out)
+        valid = len_ref[jnp.clip(place.my_seq, 0, seq_count - 1)]
+        position = lax.broadcasted_iota(jnp.int32, bias_ref.shape, 1)
+        bias_ref[...] = jnp.where(position < valid, 0.0, 8.0 * NEG_FILL)
 
     x_rows = x_ref[...]
     depth = x_rows.shape[1]
+    column = pl.ds(pl.multiple_of(step * LANES, LANES), LANES)
     mats = [ref[...].reshape(depth, LANES) for ref in (wq_ref, wk_ref, wv_ref)]
     both = dot(x_rows, jnp.concatenate(mats, axis=1), 1, 0)
-    q_ref[...] = (both[:, :LANES] + bq_ref[...]).astype(BF16)
+    q_ref[...] = (both[:, :LANES] + vec_out[BQ : BQ + 1, column]).astype(BF16)
     k_ref[...] = both[:, LANES : 2 * LANES].astype(BF16)
-    v_ref[...] = (both[:, 2 * LANES :] + bv_ref[...]).astype(BF16)
+    v_ref[...] = (both[:, 2 * LANES :] + vec_out[BV : BV + 1, column]).astype(BF16)
     attend_kernel(bias_ref, q_ref, k_ref, v_ref, ctx_ref, probs_ref, rows_blk=rows_blk)
 
     @pl.when(step == last - 1)
@@ -427,7 +466,7 @@
         rows.finish()
 
 
-def forward_all(seq_size, bias, rows, qkv_full, bq, bv, upstream, w2_full, w1_full, wo_full):
+def forward_all(seq_size, lengths, rows, qkv_full, vec_full, upstream, w2_full, w1_full, wo_full):
     seq_len, feats = rows.shape
     seq_count, blk, _ = upstream.shape
     pairs = feats // LANES
@@ -439,48 +478,161 @@
     def mat(which):
         return pl.BlockSpec((8, shard, LANES), lambda g, w=which: (0, 0, w * pairs + g))
 
-    vec = pl.BlockSpec((1, LANES), lambda g: (0, g))
     fulls = [w2_full, w1_full, wo_full]
     flat = jax.ShapeDtypeStruct((seq_len, feats), BF16)
     return pl.pallas_call(
         functools.partial(forward_kernel, seq_size, seq_count, min(512, seq_len)),
         grid=(pairs,),
         in_specs=[
-            pl.BlockSpec((1, seq_len), lambda g: (0, 0)),
+            pl.BlockSpec(memory_space=pltpu.SMEM),
             pl.BlockSpec((seq_len, feats), lambda g: (0, 0)),
-            mat(0), mat(1), mat(2), vec, vec,
+            mat(0), mat(1), mat(2), pl.BlockSpec(vec_full.shape, lambda g: (0, 0, 0)),
         ]
         + [any_spec] * 4,
         out_specs=[cols] * 4
-        + [pl.BlockSpec((2, seq_len, seq_len), lambda g: (g, 0, 0))]
+        + [
+            pl.BlockSpec((2, seq_len, seq_len), lambda g: (g, 0, 0)),
+            pl.BlockSpec((16, feats), lambda g: (0, 0)),
+        ]
         + [any_spec] * 4,
         out_shape=[flat] * 4
-        + [jax.ShapeDtypeStruct((feats // HEAD, seq_len, seq_len), BF16), flat]
+        + [
+            jax.ShapeDtypeStruct((feats // HEAD, seq_len, seq_len), BF16),
+            jax.ShapeDtypeStruct((16, feats), F32),
+            flat,
+        ]
         + [jax.ShapeDtypeStruct(item.shape, BF16) for item in fulls],
         scratch_shapes=[
-            pltpu.VMEM((blk, feats), BF16),
+            pltpu.VMEM((1, seq_len), F32), pltpu.VMEM((blk, feats), BF16),
             dma((seq_count,)), dma((seq_size,)), dma((seq_size,)),
             dma((3, 6)), dma((3, 6)), dma((3, 7)), dma((3, 7)),
         ],
-        input_output_aliases={8: 6, 9: 7, 10: 8},
+        input_output_aliases={7: 7, 8: 8, 9: 9},
         compiler_params=pltpu.CompilerParams(
             collective_id=3, has_side_effects=True, vmem_limit_bytes=VMEM_LIMIT
         ),
-    )(bias, rows, qkv_full, qkv_full, qkv_full, bq, bv, upstream, *fulls)
+    )(lengths, rows, qkv_full, qkv_full, qkv_full, vec_full, upstream, *fulls)
+
+
+def add_rows(dest, first, *others, start=0, count=None):
+    count = dest.shape[0] if count is None else count
+
+    def body(i, carry):
+        to = pl.ds(pl.multiple_of(start + i * 16, 16), 16)
+        frm = pl.ds(pl.multiple_of(i * 16, 16), 16)
+        if len(others) == 1:
+            dest[to, :] = first[to, :] + others[0][frm, :]
+        else:
+            value = first[to, :].astype(F32)
+            for other in others:
+                value = value + other[frm, :].astype(F32)
+            dest[to, :] = value.astype(dest.dtype)
+        return carry
+
+    lax.fori_loop(0, count // 16, body, 0, unroll=True)
+
+
+class Chain:
+    def __init__(self, place, mine, passed, arrived, total, sems, index):
+        self.place, self.mine, self.passed, self.arrived = place, mine, passed, arrived
+        self.total, self.index = total, index
+        self.z_send, self.z_recv = sems
+
+    def copy(self, way, src):
+        at = self.place
+        return remote(
+            src, self.arrived.at[way], self.z_send.at[self.index, way],
+            self.z_recv.at[self.index, way], (at.me, at.here + (1, -1)[way]),
+        )
+
+    def hops(self, way):
+        at = self.place
+        return at.here if way == 0 else at.seq_size - 1 - at.here
+
+    def hop(self, hop):
+        for way in range(2):
+            passed = self.passed.at[way]
+
+            @pl.when(self.hops(way) == hop)
+            def _():
+                if hop == 0:
+                    self.copy(way, self.mine).start()
+                else:
+                    self.copy(way, passed).wait_recv()
+                    if hop < self.place.seq_size - 1:
+                        add_rows(passed, self.mine, self.arrived.at[way])
+                        self.copy(way, passed).start()
+
+    def finish(self):
+        last = self.place.seq_size - 1
+        up, down = self.arrived.at[0], self.arrived.at[1]
+        here = self.place.here
+
+        @pl.when(here == 0)
+        def _():
+            add_rows(self.total, self.mine, down)
+
+        @pl.when(here == last)
+        def _():
+            add_rows(self.total, self.mine, up)
+
+        @pl.when((here > 0) & (here < last))
+        def _():
+            add_rows(self.total, self.mine, up, down)
+
+    def drain(self):
+        for way in range(2):
+
+            @pl.when(self.hops(way) < self.place.seq_size - 1)
+            def _():
+                self.copy(way, self.mine).wait_send()
+
+    @staticmethod
+    def semaphores(count):
+        dma = pltpu.SemaphoreType.DMA
+        return [dma((count, 2)), dma((count, 2))]
+
+
+class Carried:
+    def __init__(self, place, source, result, bufs, sems, copy_sems, index, slot):
+        mine, passed, arrived, total = bufs
+        self.chain = Chain(place, mine, passed, arrived, total, sems, index)
+        self.load = pltpu.make_async_copy(source, mine, copy_sems.at[slot, 0])
+        self.out = pltpu.make_async_copy(total, result, copy_sems.at[slot, 1])
+
+    def begin(self):
+        self.load.wait()
+        self.chain.hop(0)
+
+    def hop(self, hop):
+        self.chain.hop(hop)
+
+    def finish(self):
+        self.chain.finish()
+        self.out.start()
+
+    def drain(self):
+        self.chain.drain()
+        self.out.wait()
 
 
 class Reduce:
-    def __init__(self, place, source, total, bufs, sems, index):
-        self.place, self.source, self.total, self.index = place, source, total, index
-        self.own, self.other, self.first_x, self.first_y, self.second, self.arrived = bufs
+    def __init__(self, place, source, result, bufs, sems, index, z_arrived=None, z_sems=None):
+        self.place, self.source, self.index = place, source, index
+        self.own, self.other, self.first_x, self.first_y, self.second = bufs
         (
             self.own_sem, self.core_send, self.core_recv, self.one_send, self.one_recv,
-            self.two_send, self.two_recv, self.z_send, self.z_recv,
+            self.two_send, self.two_recv,
         ) = sems
         at = place
         self.apart = [(r % 2) * at.to_x + (r // 2) * at.to_y for r in range(4)]
         self.rows = self.own.shape[1]
         self.half = self.rows // 2
+        self.chain, total = None, self.own.at[0]
+        if z_arrived is not None:
+            total = self.own.at[3]
+            self.chain = Chain(place, self.own.at[0], self.other, z_arrived, total, z_sems, index)
+        self.out = pltpu.make_async_copy(total, result, self.own_sem.at[index, 3])
 
     def keep_copy(self, r):
         return pltpu.make_async_copy(
@@ -513,34 +665,6 @@
             self.two_recv.at[self.index, way], (self.place.y_dev, self.place.x_dev)[way],
         )
 
-    def z_copy(self, way, src):
-        at = self.place
-        return remote(
-            src, self.arrived.at[way], self.z_send.at[self.index, way],
-            self.z_recv.at[self.index, way], (at.me, at.here + (1, -1)[way]),
-        )
-
-    def hops(self, way):
-        at = self.place
-        return at.here if way == 0 else at.seq_size - 1 - at.here
-
-    def add(self, dest, first, *others, start=0, count=None):
-        count = self.rows if count is None else count
-
-        def body(i, carry):
-            to = pl.ds(pl.multiple_of(start + i * 16, 16), 16)
-            frm = pl.ds(pl.multiple_of(i * 16, 16), 16)
-            if len(others) == 1:
-                dest[to, :] = first[to, :] + others[0][frm, :]
-            else:
-                value = first[to, :].astype(F32)
-                for other in others:
-                    value = value + other[frm, :].astype(F32)
-                dest[to, :] = value.astype(dest.dtype)
-            return carry
-
-        lax.fori_loop(0, count // 16, body, 0, unroll=True)
-
     def begin(self):
         for r in (3, 1, 2, 0):
             self.core_copy(r).start()
@@ -550,7 +674,7 @@
         for r in (3, 1, 2, 0):
             self.keep_copy(r).wait()
             self.core_copy(r).wait_recv()
-            self.add(self.own.at[r], self.own.at[r], self.other.at[r])
+            add_rows(self.own.at[r], self.own.at[r], self.other.at[r])
             if r == 3:
                 self.one_copy(0, 1).start()
                 self.one_copy(1, 1).start()
@@ -565,7 +689,7 @@
             for way in range(2):
                 self.one_copy(way, k).wait_recv()
                 dest = self.own.at[(2, 1)[way] if k else 0]
-                self.add(dest, dest, firsts[way].at[k], start=way * self.half, count=self.half)
+                add_rows(dest, dest, firsts[way].at[k], start=way * self.half, count=self.half)
                 if k:
                     self.two_copy(way).start()
 
@@ -573,70 +697,37 @@
         mine = self.own.at[0]
         for way in range(2):
             self.two_copy(way).wait_recv()
-            self.add(mine, mine, self.second.at[way], start=way * self.half, count=self.half)
-        self.z_hop(0)
-
-    def z_hop(self, hop):
-        mine = self.own.at[0]
-        for way in range(2):
-            passed = self.other.at[way]
-
-            @pl.when(self.hops(way) == hop)
-            def _():
-                if hop == 0:
-                    self.z_copy(way, mine).start()
-                else:
-                    self.z_copy(way, passed).wait_recv()
-                    if hop < self.place.seq_size - 1:
-                        self.add(passed, mine, self.arrived.at[way])
-                        self.z_copy(way, passed).start()
+            add_rows(mine, mine, self.second.at[way], start=way * self.half, count=self.half)
+        if self.chain is not None:
+            self.chain.hop(0)
+
+    def hop(self, hop):
+        self.chain.hop(hop)
 
     def finish(self):
-        total = self.own.at[3]
-        last = self.place.seq_size - 1
-        mine = self.own.at[0]
-        up, down = self.arrived.at[0], self.arrived.at[1]
-        here = self.place.here
-        self.one_copy(0, 1).wait_send()
-        self.one_copy(1, 1).wait_send()
-
-        @pl.when(here == 0)
-        def _():
-            self.add(total, mine, down)
-
-        @pl.when(here == last)
-        def _():
-            self.add(total, mine, up)
-
-        @pl.when((here > 0) & (here < last))
-        def _():
-            self.add(total, mine, up, down)
-
-        self.total_copy().start()
-
-    def total_copy(self):
-        return pltpu.make_async_copy(
-            self.own.at[3], self.total, self.own_sem.at[self.index, 3]
-        )
+        if self.chain is not None:
+            self.one_copy(0, 1).wait_send()
+            self.one_copy(1, 1).wait_send()
+            self.chain.finish()
+        self.out.start()
 
     def drain(self):
         for r in range(4):
             self.core_copy(r).wait_send()
         for way in range(2):
             self.one_copy(way, 0).wait_send()
+            if self.chain is None:
+                self.one_copy(way, 1).wait_send()
             self.two_copy(way).wait_send()
-
-            @pl.when(self.hops(way) < self.place.seq_size - 1)
-            def _():
-                self.z_copy(way, self.own.at[0]).wait_send()
-
-        self.total_copy().wait()
+        if self.chain is not None:
+            self.chain.drain()
+        self.out.wait()
 
     @staticmethod
     def scratch(count, rows, width):
         return [
             pltpu.VMEM((count, lead, rows // split, width), BF16)
-            for lead, split in ((4, 1), (4, 1), (2, 2), (2, 2), (2, 2), (2, 1))
+            for lead, split in ((4, 1), (4, 1), (2, 2), (2, 2), (2, 2))
         ]
 
     @staticmethod
@@ -645,7 +736,6 @@
         return [
             dma((count, 4)), dma((count, 4)), dma((count, 4)),
             dma((count, 2, 2)), dma((count, 2, 2)), dma((count, 2)), dma((count, 2)),
-            dma((count, 2)), dma((count, 2)),
         ]
 
 
@@ -704,7 +794,6 @@
 
 INV_SQRT2 = 0.7071067811865476
 INV_SQRT_2PI = 0.3989422804014327
-BQ, BV, BO, G1, B1, C2, G2, B2, C1 = range(9)
 
 
 def normalize(resid):
@@ -828,11 +917,11 @@
 
     act_ref, slope_ref, w1_ref, w2_ref, resid_ref, normed_ref, inv_ref, ctx_ref = take(8)
     wo_ref, vec_ref, vec_in, out_rows = take(4)
-    d_w1, resid_out, grad_ctx, d_wo, vec_out, w2_total, out_blocks = take(7)
+    d_w1, resid_out, grad_ctx, d_wo, vec_out, w2_part, out_blocks = take(7)
     grad_ffn, hidden_low, d_w2, vec_sums = take(4)
     count = 4
-    bufs = take(6)
-    sems = take(9)
+    bufs = take(5)
+    sems = take(7)
     out_sems = take(3)
 
     step = pl.program_id(0)
@@ -844,7 +933,7 @@
     jobs = [
         Reduce(
             place, lambda shard, c=c: d_w2.at[shard, pl.ds(c * chunk, chunk)],
-            w2_total.at[pl.ds(c * chunk, chunk)], [buf.at[c] for buf in bufs], sems, c,
+            w2_part.at[pl.ds(c * chunk, chunk)], [buf.at[c] for buf in bufs], sems, c,
         )
         for c in range(count)
     ]
@@ -917,9 +1006,7 @@
 
     @pl.when(step == pl.num_programs(0) - 1)
     def _():
-        for job in jobs[1:]:
-            job.two_stage()
-        jobs[0].z_hop(1)
+        jobs[1].two_stage()
         merge = wo_ref[...].reshape(feats, feats)
         sums = [jnp.zeros((1, feats), F32)] * 3
         outer = jnp.zeros((feats, feats), F32)
@@ -936,8 +1023,6 @@
                 total + jnp.sum(term, axis=0, keepdims=True) for total, term in zip(sums, terms)
             ]
         d_wo[...] = outer.astype(BF16).reshape(d_wo.shape)
-        jobs[1].z_hop(1)
-        jobs[0].z_hop(2)
         row = lax.broadcasted_iota(jnp.int32, (16, 1), 0)
         lines = sums + [vec_in[k : k + 1, :] for k in range(3)]
         lines = lines + [vec_sums[k : k + 1, :] for k in range(4)]
@@ -946,13 +1031,11 @@
             packed = jnp.where(row == k, line, packed)
         vec_out[...] = packed.astype(BF16)
 
-        tail = [functools.partial(Reduce.z_hop, hop=hop) for hop in range(1, seq_size)]
-        tail.append(Reduce.finish)
-        plan = [(job, max(0, k - 1), tail[max(0, 2 - k) :]) for k, job in enumerate(jobs)]
-        for time in range(max(wait + len(stages) for _, wait, stages in plan)):
-            for job, wait, stages in plan:
-                if 0 <= time - wait < len(stages):
-                    stages[time - wait](job)
+        for job in jobs[:2]:
+            job.finish()
+        for job in jobs[2:]:
+            job.two_stage()
+            job.finish()
         for job in jobs:
             job.drain()
         outs.finish()
@@ -1019,6 +1102,10 @@
     )
 
 
+def pair_column(feats, which, pair):
+    return (pair // 2) * feats + (pair % 2) * 3 * LANES + which * LANES
+
+
 def backward_kernel(seq_size, seq_count, rows_blk, *refs):
     refs = list(refs)
 
@@ -1028,20 +1115,24 @@
         return got
 
     q_ref, k_ref, v_ref, ctx_ref, grad_ref, probs_ref, vec_ref = take(7)
-    x_in, qkv_in, resid_in, d_w1, d_wo = take(5)
-    w1_total, wo_total, wq_total, wk_total, wv_total, vec_total, token_out = take(7)
-    key_acc, value_acc, grads_all, x_rows, qkv_mat, resid, token_rows = take(7)
-    mats = take(3)
-    (vec_src,) = take(1)
+    x_in, qkv_in, resid_in, d_w1, d_wo, w2_part = take(6)
+    w2_total, w1_total, wo_total, qkv_total, vec_total, token_out = take(6)
+    key_acc, value_acc, grads, x_rows, qkv_mat, resid, token_rows = take(7)
+    mats, bias_rows, vec_src = take(3)
     w1_count = d_w1.shape[0]
     mat_count = w1_count + 4
-    bufs = take(6)
-    vec_bufs = take(6)
-    sems = take(9)
-    (load_sem,) = take(1)
+    bufs = take(5)
+    (arrived,) = take(1)
+    vec_bufs = take(5)
+    (vec_arrived,) = take(1)
+    carried_bufs = take(4)
+    sems = take(7)
+    z_sems = take(2)
+    load_sem, carried_sems = take(2)
     token_sems = take(3)
 
     step = pl.program_id(0)
+    last = pl.num_programs(0) - 1
     place = Place(seq_size, seq_count)
     seq_len, feats = x_rows.shape
 
@@ -1050,21 +1141,35 @@
             return lambda shard: d_w1.at[c, shard]
         if c == w1_count:
             return lambda shard: d_wo.at[shard]
-        return lambda shard: mats[c - w1_count - 1].at[shard]
-
-    outer_totals = [w1_total.at[:, pl.ds(c * feats, feats)] for c in range(w1_count)]
-    outer_totals += [wo_total, wq_total, wk_total, wv_total]
+        return lambda shard: mats.at[c - w1_count - 1, shard]
+
+    totals = [w1_total.at[:, pl.ds(c * feats, feats)] for c in range(w1_count)]
+    totals += [wo_total] + [qkv_total.at[:, pl.ds(c * feats, feats)] for c in range(3)]
     jobs = [
-        Reduce(place, outer_source(c), outer_totals[c], [buf.at[c] for buf in bufs], sems, c)
+        Reduce(
+            place, outer_source(c), totals[c], [buf.at[c] for buf in bufs], sems, c,
+            arrived.at[c], z_sems,
+        )
         for c in range(mat_count)
     ]
     jobs.append(
         Reduce(
             place, lambda shard: vec_src.at[shard], vec_total, [buf.at[0] for buf in vec_bufs],
-            sems, mat_count,
+            sems, mat_count, vec_arrived.at[0], z_sems,
         )
     )
-    ready = w1_count + 1
+    chunk = w2_part.shape[0] // 4
+    carried = []
+    for c in range(4):
+        rows = pl.ds(c * chunk, chunk)
+        carried.append(
+            Carried(
+                place, w2_part.at[rows], w2_total.at[rows], [buf.at[c] for buf in carried_bufs],
+                z_sems, carried_sems, mat_count + 1 + c, c,
+            )
+        )
+    w0, w1, w2, w3, wo, qkv_a, qkv_b, qkv_c, vec = jobs
+    t0, t1, t2, t3 = carried
     blk = seq_len // seq_size
     loads = [
         pltpu.make_async_copy(src, dst, load_sem.at[k])
@@ -1072,156 +1177,235 @@
     ]
     tokens = RowsOut(place, token_rows, token_out, token_sems)
 
+    core, one, two = Reduce.core_stage, Reduce.one_stage, Reduce.two_stage
+
+    def hop1(job):
+        job.hop(1)
+
+    def hop2(job):
+        job.hop(2)
+
+    def end(job):
+        job.hop(3)
+        job.finish()
+
+    ticks = (
+        ((core, w0), (core, w1)),
+        ((core, w2), (hop1, t0)),
+        ((one, w0), (hop1, t1)),
+        ((one, w1), (core, w3), (hop1, t2), (hop2, t0)),
+        ((one, w2), (hop1, t3), (hop2, t1)),
+        ((two, w0), (two, w1), (core, wo), (hop2, t2), (end, t0)),
+        ((one, w3), (core, qkv_a), (hop2, t3), (end, t1)),
+        ((two, w2), (hop1, w0), (end, t2)),
+        ((one, wo), (hop1, w1), (end, t3)),
+        ((two, w3), (core, qkv_b), (one, qkv_a), (hop1, w2), (hop2, w0)),
+        ((two, wo), (hop2, w1)),
+        ((one, qkv_b), (hop1, w3), (hop2, w2), (end, w0)),
+    )
+    after = (
+        ((two, qkv_a), (end, w1)),
+        ((core, qkv_c), (hop1, wo)),
+        ((core, vec), (two, qkv_b), (hop2, w3)),
+        ((end, w2), (hop1, qkv_a)),
+    )
+    rest = (
+        (one, qkv_c), (one, vec), (hop2, wo), (hop1, qkv_b), (end, w3),
+        (two, qkv_c), (two, vec), (hop2, qkv_a), (end, wo),
+        (hop1, qkv_c), (hop1, vec), (hop2, qkv_b), (end, qkv_a),
+        (hop2, qkv_c), (hop2, vec), (end, qkv_b),
+        (end, qkv_c), (end, vec),
+    )
+
     @pl.when(step == 0)
     def _():
         place.barrier()
-        for job in jobs[:ready]:
+        for job in carried:
+            job.load.start()
+        for job in (w0, w1, w2, w3, wo):
             job.begin()
         for load in loads:
             load.start()
-        jobs[0].core_stage()
-
-    column = pl.multiple_of(step * LANES, LANES)
+        for job in carried:
+            job.begin()
+
+    @pl.when(step == 2)
+    def _():
+        qkv_a.begin()
+
+    @pl.when(step == 4)
+    def _():
+        qkv_b.begin()
 
     def store(which, rows, values):
-        grads_all[which, rows, pl.ds(column, LANES)] = values
+        grads[rows, which * LANES : (which + 1) * LANES] = values
+
+    def between(half):
+        for at_step in range(len(ticks) // 2):
+
+            @pl.when(step == at_step)
+            def _():
+                for stage, job in ticks[2 * at_step + half]:
+                    stage(job)
 
     attend_back_pair(
-        q_ref, k_ref, v_ref, ctx_ref, grad_ref, probs_ref, store, key_acc, value_acc, rows_blk
+        q_ref, k_ref, v_ref, ctx_ref, grad_ref, probs_ref, store, key_acc, value_acc, rows_blk,
+        between,
     )
 
-    core, one, two = Reduce.core_stage, Reduce.one_stage, Reduce.two_stage
-    hops = [functools.partial(Reduce.z_hop, hop=hop) for hop in range(1, seq_size)]
-    tail = hops + [Reduce.finish]
-    ticks = (
-        ((core, 1), (core, 2)),
-        ((one, 0), (core, 3), (core, 4)),
-        ((one, 1), (one, 2)),
-        ((two, 0), (one, 3)),
-        ((two, 1), (two, 2), (one, 4), (hops[0], 0)),
-    )
-    for at_step, stages in enumerate(ticks):
-
-        @pl.when(step == at_step)
-        def _():
-            for stage, chunk in stages:
-                stage(jobs[chunk])
-
-    @pl.when(step == pl.num_programs(0) - 1)
+    @pl.when(step == 0)
     def _():
         for load in loads:
             load.wait()
-        for chunk in (3, 4):
-            two(jobs[chunk])
-        hops[0](jobs[1])
-        hops[0](jobs[2])
-        hops[1](jobs[0])
-        after = (
-            ((hops[0], 3), (hops[1], 1), (hops[2], 0)),
-            ((hops[0], 4), (hops[1], 2), (hops[2], 1), (Reduce.finish, 0)),
-            ((hops[1], 3), (hops[2], 2), (Reduce.finish, 1)),
-            ((hops[1], 4), (hops[2], 3), (Reduce.finish, 2)),
-        )
+
+    width = 3 * LANES
+    column = pl.multiple_of(step * LANES, LANES)
+    half = pl.multiple_of((step % 2) * width, LANES)
+    outer = dot(x_rows[...], grads[...], 0, 0).astype(BF16)
+    mats[step // 2, :, :, pl.ds(half, width)] = outer.reshape(8, feats // 8, width)
+    sums = dot(jnp.ones((16, seq_len), BF16), grads[...], 1, 0)
+    bias_rows[0, :, pl.ds(column, LANES)] = sums[:, :LANES]
+    bias_rows[1, :, pl.ds(column, LANES)] = sums[:, 2 * LANES :]
+    mat = jnp.concatenate(
+        [
+            qkv_mat[:, :, pl.ds(pl.multiple_of(which * feats + column, LANES), LANES)].reshape(
+                feats, LANES
+            )
+            for which in range(3)
+        ],
+        axis=1,
+    )
+
+    @pl.when(step < last)
+    def _():
         for pos in range(seq_size):
             rows = pl.ds(pos * blk, blk)
-            part = resid[rows, :]
-            for which in range(3):
-                mat = qkv_mat[:, :, which * feats : (which + 1) * feats].reshape(feats, feats)
-                part = part + dot(grads_all[which, rows, :], mat, 1, 1)
-            token_rows[rows, :] = part.astype(BF16)
-            tokens.start(pos)
-            for stage, chunk in after[pos]:
-                stage(jobs[chunk])
-        for which in range(3):
-            outer_sum = dot(x_rows[...], grads_all[which], 0, 0).astype(BF16)
-            mats[which][...] = outer_sum.reshape(mats[which].shape)
-            jobs[ready + which].begin()
-            if which:
-                core(jobs[ready + which - 1])
-        ones = jnp.ones((16, seq_len), BF16)
-        grad_bq = dot(ones, grads_all[0], 1, 0)
-        grad_bv = dot(ones, grads_all[2], 1, 0)
+            resid[rows, :] += dot(grads[rows, :], mat, 1, 1)
+
+    @pl.when(step == last)
+    def _():
+        qkv_c.begin()
         row = lax.broadcasted_iota(jnp.int32, (16, 1), 0)
-        biases = jnp.where(row == 0, grad_bq, grad_bv).astype(BF16)
+        biases = jnp.where(row == 0, bias_rows[0], bias_rows[1]).astype(BF16)
         for shard in range(8):
             vec_src[shard, 0:16, :] = vec_ref[...]
             vec_src[shard, 16:32, :] = biases
-        jobs[-1].begin()
-        core(jobs[-2])
-        core(jobs[-1])
-
-        plan = [(jobs[3], 0, [Reduce.finish]), (jobs[4], 0, tail[2:])]
-        for k, job in enumerate(jobs[ready:]):
-            plan.append((job, k, [one, two] + tail))
-        for time in range(max(wait + len(stages) for _, wait, stages in plan)):
-            for job, wait, stages in plan:
-                if 0 <= time - wait < len(stages):
-                    stages[time - wait](job)
-        for job in jobs:
+        vec.begin()
+        for pos in range(seq_size):
+            rows = pl.ds(pos * blk, blk)
+            total = resid[rows, :] + dot(grads[rows, :], mat, 1, 1)
+            token_rows[rows, :] = total.astype(BF16)
+            tokens.start(pos)
+            for stage, job in after[pos]:
+                stage(job)
+        for stage, job in rest:
+            stage(job)
+        for job in jobs + carried:
             job.drain()
         tokens.finish()
 
 
 def backward_all(
     seq_size, seq_count, query, key, value, ctx, grad_ctx, probs, vecs, inputs, qkv_full, resid,
-    d_w1, d_wo,
+    d_w1, d_wo, w2_part,
 ):
     seq_len, feats = ctx.shape
     blk = seq_len // seq_size
     shard = qkv_full.shape[1]
     w1_count = d_w1.shape[0]
     count = w1_count + 4
+    chunk = w2_part.shape[0] // 4
     any_spec = pl.BlockSpec(memory_space=pl.ANY)
     cols = pl.BlockSpec((seq_len, LANES), lambda g: (0, g))
     dma = pltpu.SemaphoreType.DMA
-    mat = jax.ShapeDtypeStruct((shard, feats), BF16)
+
+    def low(*shape):
+        return jax.ShapeDtypeStruct(shape, BF16)
+
     return pl.pallas_call(
-        functools.partial(backward_kernel, seq_size, seq_count, min(512, seq_len)),
+        functools.partial(backward_kernel, seq_size, seq_count, seq_len // 2),
         grid=(feats // LANES,),
         in_specs=[cols] * 5
         + [
             pl.BlockSpec((2, seq_len, seq_len), lambda g: (g, 0, 0)),
             pl.BlockSpec(vecs.shape, lambda g: (0, 0)),
         ]
-        + [any_spec] * 5,
-        out_specs=[any_spec] * 7,
-        out_shape=[jax.ShapeDtypeStruct((shard, w1_count * feats), BF16), mat, mat, mat, mat]
-        + [
-            jax.ShapeDtypeStruct((32, feats), BF16),
-            jax.ShapeDtypeStruct((seq_count, blk, feats), BF16),
+        + [any_spec] * 6,
+        out_specs=[any_spec] * 6,
+        out_shape=[
+            low(*w2_part.shape), low(shard, w1_count * feats), low(shard, feats),
+            low(shard, 3 * feats), low(32, feats), low(seq_count, blk, feats),
         ],
         scratch_shapes=[pltpu.VMEM((2, HEAD, seq_len), F32)] * 2
         + [
-            pltpu.VMEM((3, seq_len, feats), BF16),
+            pltpu.VMEM((seq_len, 3 * LANES), BF16),
             pltpu.VMEM((seq_len, feats), BF16),
             pltpu.VMEM(qkv_full.shape, BF16),
             pltpu.VMEM((seq_len, feats), F32),
             pltpu.VMEM((seq_len, feats), BF16),
+            pltpu.VMEM((3, 8, shard, feats), BF16),
+            pltpu.VMEM((2, 16, feats), F32),
+            pltpu.VMEM((8, 32, feats), BF16),
         ]
-        + [pltpu.VMEM((8, shard, feats), BF16)] * 3
-        + [pltpu.VMEM((8, 32, feats), BF16)]
         + Reduce.scratch(count, shard, feats)
+        + [pltpu.VMEM((count, 2, shard, feats), BF16)]
         + Reduce.scratch(1, 32, feats)
+        + [pltpu.VMEM((1, 2, 32, feats), BF16)]
+        + [
+            pltpu.VMEM((4, chunk, feats), BF16), pltpu.VMEM((4, 2, chunk, feats), BF16),
+            pltpu.VMEM((4, 2, chunk, feats), BF16), pltpu.VMEM((4, chunk, feats), BF16),
+        ]
         + Reduce.semaphores(count + 1)
-        + [dma((3,)), dma((seq_size,)), dma((seq_count,)), dma((1,))],
+        + Chain.semaphores(count + 5)
+        + [dma((3,)), dma((4, 2)), dma((seq_size,)), dma((seq_count,)), dma((1,))],
         compiler_params=pltpu.CompilerParams(
             collective_id=1, has_side_effects=True, vmem_limit_bytes=VMEM_MAX
         ),
-    )(query, key, value, ctx, grad_ctx, probs, vecs, inputs, qkv_full, resid, d_w1, d_wo)
-
-
-def widen_kernel(*refs):
-    count = len(refs) // 2
-    for source, dest in zip(refs[:count], refs[count:]):
-        dest[...] = source[...].astype(F32)
-
-
-def widen(arrays):
+    )(
+        query, key, value, ctx, grad_ctx, probs, vecs, inputs, qkv_full, resid, d_w1, d_wo, w2_part
+    )
+
+
+def widen_kernel(w2_in, w1_in, wo_in, qkv_in, vec_in, *outs):
+    w2_out, w1_out, wo_out = outs[:3]
+    mats, vecs = outs[3:6], outs[6:]
+    feats = wo_in.shape[1]
+    w2_out[...] = w2_in[...].astype(F32)
+    w1_out[...] = w1_in[...].astype(F32)
+    wo_out[...] = wo_in[...].astype(F32)
+    for which, mat in enumerate(mats):
+        for pair in range(feats // LANES):
+            start = pair_column(feats, which, pair)
+            mat[:, pair * LANES : (pair + 1) * LANES] = qkv_in[:, start : start + LANES].astype(F32)
+    me = lax.axis_index("dp")
+    part = feats // 8
+    rows = vec_in[...].astype(F32)
+    own = jnp.zeros((rows.shape[0], part), F32)
+    long = jnp.zeros((1, 4 * part), F32)
+    for k in range(8):
+        own = jnp.where(me == k, rows[:, k * part : (k + 1) * part], own)
+        row, start = 6 + k // 2, (k % 2) * 4 * part
+        long = jnp.where(me == k, rows[row : row + 1, start : start + 4 * part], long)
+    for k, row in enumerate((16, 17, 2, 0, 1, 5, 3, 4)):
+        vecs[k][...] = own[row : row + 1, :]
+    vecs[8][...] = long
+
+
+def widen(w2_sum, w1_sum, wo_sum, qkv_sum, vec_sum):
+    feats = wo_sum.shape[1]
+    part = feats // 8
+
+    def wide(*shape):
+        return jax.ShapeDtypeStruct(shape, F32)
+
     return pl.pallas_call(
         widen_kernel,
-        out_shape=[jax.ShapeDtypeStruct(item.shape, F32) for item in arrays],
+        out_shape=[wide(*w2_sum.shape), wide(*w1_sum.shape)]
+        + [wide(*wo_sum.shape)] * 4
+        + [wide(1, part)] * 8
+        + [wide(1, 4 * part)],
         compiler_params=pltpu.CompilerParams(vmem_limit_bytes=VMEM_LIMIT),
-    )(*arrays)
+    )(w2_sum, w1_sum, wo_sum, qkv_sum, vec_sum)
 
 
 def column_sum(rows):
@@ -1286,61 +1470,48 @@
 
     wq, bq, wk, wv, bv, wo, bo, g1, b1, w1, c1, w2, c2, g2, b2 = weights
     shard_rows = feats // dp_size
-    direct = dp_size == 8 and shard_rows % 32 == 0
+    seq_len = seq_size * row_count
+    direct = (dp_size, seq_size, feats, seq_len) == (8, 4, 768, 1024) and seq_count == 3
     vec_parts = (bq, bv, bo, g1, b1, c2, g2, b2, c1)
     vec_sizes = [item.shape[0] for item in vec_parts]
     vec_len = sum(vec_sizes)
-    vec_rows = -(-vec_len // (32 * LANES)) * 32
-    packed = jnp.concatenate(vec_parts).astype(BF16)
-    seq_len = seq_size * row_count
-    position = lax.iota(jnp.int32, seq_len)
-    valid_len = lax.dynamic_index_in_dim(lengths, my_seq, 0, keepdims=False)
-    key_bias = jnp.where(position < valid_len, 0.0, 8.0 * NEG_FILL).astype(F32).reshape(1, seq_len)
-
-    if direct:
-        packed = jnp.pad(packed, (0, vec_rows * LANES - vec_len)).reshape(vec_rows, LANES)
-        inputs, qkv_full, packed, w2_part, w1_part, wo_part = start_all(
-            seq_size, tokens, (wq, wk, wv), packed, w2, w1, wo
-        )
-        packed = packed.reshape(dp_size, vec_rows * LANES)
-        qkv_mat = qkv_full.reshape(feats, 3 * feats)
-    else:
+    if not direct:
+        packed = jnp.concatenate(vec_parts).astype(BF16)
+        position = lax.iota(jnp.int32, seq_len)
+        valid_len = lax.dynamic_index_in_dim(lengths, my_seq, 0, keepdims=False)
+        key_bias = jnp.where(position < valid_len, 0.0, 8.0 * NEG_FILL).astype(F32)
+        key_bias = key_bias.reshape(1, seq_len)
         qkv_mat = gather(jnp.concatenate([wq, wk, wv], axis=1).astype(BF16))
         packed = lax.all_gather(packed, "dp", axis=0, tiled=False)
         merge_mat, expand_mat, reduce_mat = [gather(item.astype(BF16)) for item in (wo, w1, w2)]
-    vecs = []
-    start = 0
-    for size in vec_sizes:
-        vecs.append(packed[:, start : start + size].reshape(1, -1).astype(F32))
-        start += size
-    bq, bv, bo, g1, b1, c2, g2, b2, c1 = vecs
+        vecs = []
+        start = 0
+        for size in vec_sizes:
+            vecs.append(packed[:, start : start + size].reshape(1, -1).astype(F32))
+            start += size
+        bq, bv, bo, g1, b1, c2, g2, b2, c1 = vecs
 
     if direct:
-        query, key, value, ctx, probs, dy, w2_full, w1_full, wo_full = forward_all(
-            seq_size, key_bias, inputs, qkv_full, bq, bv, upstream, w2_part, w1_part, wo_part
-        )
-        vec_rows = jnp.concatenate([item.reshape(-1, feats) for item in vecs])
-        vec_rows = jnp.pad(vec_rows, ((0, 16 - vec_rows.shape[0]), (0, 0)))
+        inputs, qkv_full, vec_full, w2_part, w1_part, wo_part = start_all(
+            seq_size, tokens, (wq, wk, wv), [item.reshape(1, -1) for item in vec_parts], w2, w1, wo
+        )
+        query, key, value, ctx, probs, vec_rows, dy, w2_full, w1_full, wo_full = forward_all(
+            seq_size, lengths, inputs, qkv_full, vec_full, upstream, w2_part, w1_part, wo_part
+        )
         act, slope, out_rows, grad_resid2, normed1, inv1, second_sums = feed_forward(
             ctx, inputs, wo_full, vec_rows, w1_full, w2_full, dy
         )
-        d_w1, grad_resid1, grad_ctx, d_wo, vec_sums, sum_w2, output = feed_back(
+        d_w1, grad_resid1, grad_ctx, d_wo, vec_sums, part_w2, output = feed_back(
             seq_size, seq_count, act, slope, w1_full, w2_full, grad_resid2, normed1, inv1, ctx,
             wo_full, vec_rows, second_sums, out_rows,
         )
-        *sums, vec_sum, token_grad = backward_all(
+        *sums, token_grad = backward_all(
             seq_size, seq_count, query, key, value, ctx, grad_ctx, probs, vec_sums, inputs,
-            qkv_full, grad_resid1, d_w1, d_wo,
-        )
-        sum_w2, sum_w1, s_wo, s_wq, s_wk, s_wv, vec_sum = widen([sum_w2] + sums + [vec_sum])
-
-        def own_part(first, length):
-            rows = vec_sum[first : first + -(-length * dp_size // feats)].reshape(-1)
-            return lax.dynamic_slice(rows, (dp_index * length,), (length,))
-
-        s_g1, s_b1, s_bo, s_g2, s_b2, s_c2 = [own_part(k, shard_rows) for k in range(6)]
-        s_c1 = own_part(6, c1.shape[1] // dp_size)
-        s_bq, s_bv = own_part(16, shard_rows), own_part(17, shard_rows)
+            qkv_full, grad_resid1, d_w1, d_wo, part_w2,
+        )
+        sum_w2, sum_w1, s_wo, s_wq, s_wk, s_wv, *vec_sums = widen(*sums)
+        vec_sums = [item.reshape(-1) for item in vec_sums]
+        s_bq, s_bv, s_bo, s_g1, s_b1, s_c2, s_g2, s_b2, s_c1 = vec_sums
     else:
         inputs = to_owners(tokens)
         dy = to_owners(upstream).astype(F32)

time: 335 us -> 279 us (0.83)
  Pallas kernels: 309 us -> 268 us
  local copies, waits for them, and re-layouts: 12.2 us -> 3.28 us
  other arithmetic: 7.26 us -> 1.37 us
    pallas_call x1, Pallas kernels: 75.4 us -> 54.3 us  [feed_back(): pl.pallas_call(functools.partial(feed_back_kernel, seq_size, seq_count, m...]
    pallas_call x2, Pallas kernels: 122 us -> 102 us  [the longest x1 98.1 us: backward_all(): pl.pallas_call(functools.partial(backward_kernel, seq_size, seq_count, se...]
    another operation x9 -> x0, other arithmetic: 5.94 us -> none
    dynamic_slice x6 -> x0, local copies, waits for them, and re-layouts: 4.25 us -> none  [the longest x5 3 us: own_part(): return lax.dynamic_slice(rows, (dp_index * length,), (length,))]
where the time goes in v1:
time: 279 us; the launch traced here: 274 us
  Pallas kernels  268 us (96%)
  local copies, waits for them, and re-layouts  3.28 us (1%)
    pallas_call x1, Pallas kernels, backward_all(): pl.pallas_call(functools.partial(backward_kernel, seq_size, seq_count, se...  98.1 us
    pallas_call x1, Pallas kernels, feed_back(): pl.pallas_call(functools.partial(feed_back_kernel, seq_size, seq_count, m...  54.3 us
    pallas_call x1, Pallas kernels, forward_all(): pl.pallas_call(functools.partial(forward_kernel, seq_size, seq_count, min...  42.3 us
    pallas_call x1, Pallas kernels, start_all(): pl.pallas_call(functools.partial(start_kernel, seq_size, seq_count), in_s...  39.3 us
    pallas_call x1, Pallas kernels, feed_forward(): pl.pallas_call(functools.partial(feed_kernel, min(256, seq_len)), grid=(s...  30.4 us

profile of v1, /device:TPU:0, one launch (start us, length us, event | category | flops | bytes accessed | tf_op | source)
XLA Modules:
  0.0 274.1 jit_solution(3617697759512665640)
XLA Ops:
  0.7 1.2 reshape.96.refs_8_
  1.9 39.3 %shard_map.305 = (bf16[1024,768]{1,0:T(8,128)(2,1)}, bf16[8,96,2304]{2,1,0:T(8,128)(2,1)}, bf16[8,32,128]{2,1,0:T(8,128)(2,1)}, bf16[8,384,768]{2,1,0:T(8,128)(2...) custom-call(bf16[3,256,768]{2,1,0:T(8,128)(2,1)} %tokens.1, f32[96,768]{1,0:T(8,128)} %wq.1, ...), custom_call_target="tpu_custom_call" | custom-call | tf_op jit(solution)/shard_map/pallas_call | solution.py:366
  41.2 42.3 %shard_map.306 = (bf16[1024,768]{1,0:T(8,128)(2,1)}, bf16[1024,768]{1,0:T(8,128)(2,1)}, bf16[1024,768]{1,0:T(8,128)(2,1)}, bf16[1024,768]{1,0:T(8,128)(2,1)}, bf...) custom-call(s32[3]{0:T(128)} %len_ref.1, ...), custom_call_target="tpu_custom_call", output_to_operand_aliasing={{7}: (7, {}), {8}: (8, {}), {9}: (9, {})} | custom-call | tf_op jit(solution)/shard_map/pallas_call | solution.py:483
  83.5 30.4 %shard_map.307 = (bf16[1024,3072]{1,0:T(8,128)(2,1)}, bf16[1024,3072]{1,0:T(8,128)(2,1)}, bf16[1024,768]{1,0:T(8,128)(2,1)}, f32[1024,768]{1,0:T(8,128)}, f32[10...) custom-call(bf16[1024,768]{1,0:T(8,128)(2,1)} %get-tuple-element.74.ctx_ref.refs_7_.refs_3_, ...), custom_call_target="tpu_custom_call" | custom-call | tf_op jit(solution)/shard_map/pallas_call | solution.py:889
  113.9 54.3 %shard_map.308 = (bf16[4,8,96,768]{3,2,1,0:T(8,128)(2,1)}, f32[1024,768]{1,0:T(8,128)}, bf16[1024,768]{1,0:T(8,128)(2,1)}, bf16[8,96,768]{2,1,0:T(8,128)(2,1)}, ...) custom-call(bf16[1024,3072]{1,0:T(8,128)(2,1)} %get-tuple-element.80.refs_0_, ...), custom_call_target="tpu_custom_call" | custom-call | tf_op jit(solution)/shard_map/pallas_call | solution.py:1066
  168.2 98.1 %shard_map.309 = (bf16[384,768]{1,0:T(8,128)(2,1)}, bf16[96,3072]{1,0:T(8,128)(2,1)}, bf16[96,768]{1,0:T(8,128)(2,1)}, bf16[96,2304]{1,0:T(8,128)(2,1)}, bf16[32...) custom-call(bf16[1024,768]{1,0:T(8,128)(2,1)} %get-tuple-element.88.refs_0_, bf16[1024,768]{1,0:T(8,128)(2,1)} %get-tuple-element.89.refs_1_, ...), custom_call_target="tpu_custom_call" | custom-call | tf_op jit(solution)/shard_map/pallas_call | solution.py:1325
  266.3 0.0 copy-start
  266.3 3.9 %shard_map.310 = (f32[384,768]{1,0:T(8,128)}, f32[96,3072]{1,0:T(8,128)}, f32[96,768]{1,0:T(8,128)}, f32[96,768]{1,0:T(8,128)}, f32[96,768]{1,0:T(8,128)}, /*ind...) custom-call(bf16[384,768]{1,0:T(8,128)(2,1)} %get-tuple-element.99.w, ...), custom_call_target="tpu_custom_call" | custom-call | tf_op jit(solution)/shard_map/pallas_call | solution.py:1401
  270.2 0.0 copy-start.1
  270.2 1.4 reduce
  271.6 0.0 copy-done
  271.6 1.0 copy.43
  272.6 0.0 copy-done.1
  272.6 1.0 copy.44
Async XLA Ops:
  266.3 5.3 %copy-start = (bf16[3,256,768]{2,1,0:T(8,128)(2,1)S(1)}, bf16[3,256,768]{2,1,0:T(8,128)(2,1)}, u32[]{:S(2)}) copy-start(bf16[3,256,768]{2,1,0:T(8,128)(2,1)} %get-tuple-element.136) | copy-start | bytes 3538948
  270.2 2.4 copy-start.1

commit v2 on v1

--- a/solution.py
+++ b/solution.py
@@ -516,20 +516,22 @@
 
 def add_rows(dest, first, *others, start=0, count=None):
     count = dest.shape[0] if count is None else count
+    size = 48 if count % 48 == 0 else min(count, 64)
 
     def body(i, carry):
-        to = pl.ds(pl.multiple_of(start + i * 16, 16), 16)
-        frm = pl.ds(pl.multiple_of(i * 16, 16), 16)
-        if len(others) == 1:
-            dest[to, :] = first[to, :] + others[0][frm, :]
-        else:
-            value = first[to, :].astype(F32)
-            for other in others:
-                value = value + other[frm, :].astype(F32)
-            dest[to, :] = value.astype(dest.dtype)
+        for k in range(size // 16):
+            to = pl.ds(pl.multiple_of(start + i * size + k * 16, 16), 16)
+            frm = pl.ds(pl.multiple_of(i * size + k * 16, 16), 16)
+            if len(others) == 1:
+                dest[to, :] = first[to, :] + others[0][frm, :]
+            else:
+                value = first[to, :].astype(F32)
+                for other in others:
+                    value = value + other[frm, :].astype(F32)
+                dest[to, :] = value.astype(dest.dtype)
         return carry
 
-    lax.fori_loop(0, count // 16, body, 0, unroll=True)
+    lax.fori_loop(0, count // size, body, 0, unroll=count == size)
 
 
 class Chain:
@@ -542,7 +544,7 @@
         at = self.place
         return remote(
             src, self.arrived.at[way], self.z_send.at[self.index, way],
-            self.z_recv.at[self.index, way], (at.me, at.here + (1, -1)[way]),
+            self.z_recv.at[self.index, way], (at.me, at.here + 1 - 2 * way),
         )
 
     def hops(self, way):
@@ -550,35 +552,32 @@
         return at.here if way == 0 else at.seq_size - 1 - at.here
 
     def hop(self, hop):
-        for way in range(2):
+        here, last = self.place.here, self.place.seq_size - 1
+
+        @pl.when((here == hop) | (here == last - hop))
+        def _():
+            way = jnp.where(here == hop, 0, 1)
             passed = self.passed.at[way]
-
-            @pl.when(self.hops(way) == hop)
-            def _():
-                if hop == 0:
-                    self.copy(way, self.mine).start()
-                else:
-                    self.copy(way, passed).wait_recv()
-                    if hop < self.place.seq_size - 1:
-                        add_rows(passed, self.mine, self.arrived.at[way])
-                        self.copy(way, passed).start()
+            if hop == 0:
+                self.copy(way, self.mine).start()
+            else:
+                self.copy(way, passed).wait_recv()
+                if hop < last:
+                    add_rows(passed, self.mine, self.arrived.at[way])
+                    self.copy(way, passed).start()
 
     def finish(self):
         last = self.place.seq_size - 1
-        up, down = self.arrived.at[0], self.arrived.at[1]
         here = self.place.here
-
-        @pl.when(here == 0)
+        inner = (here > 0) & (here < last)
+
+        @pl.when(jnp.logical_not(inner))
         def _():
-            add_rows(self.total, self.mine, down)
-
-        @pl.when(here == last)
+            add_rows(self.total, self.mine, self.arrived.at[jnp.where(here == 0, 1, 0)])
+
+        @pl.when(inner)
         def _():
-            add_rows(self.total, self.mine, up)
-
-        @pl.when((here > 0) & (here < last))
-        def _():
-            add_rows(self.total, self.mine, up, down)
+            add_rows(self.total, self.mine, self.arrived.at[0], self.arrived.at[1])
 
     def drain(self):
         for way in range(2):
@@ -821,7 +820,8 @@
 ):
     step = pl.program_id(0)
     seq_len, feats = x_ref.shape
-    width = act_ref.shape[1]
+    width = slope_ref.shape[1]
+    parts = act_ref.shape[0]
     blocks = [pl.ds(i * rows_blk, rows_blk) for i in range(seq_len // rows_blk)]
 
     def vec(k):
@@ -836,6 +836,7 @@
             normed_ref[rows, :] = normed
             inv_ref[rows, :] = jnp.broadcast_to(inv, (rows_blk, LANES))
             hidden_low[rows, :] = (normed * vec(G1) + vec(B1)).astype(BF16)
+            resid_ref[rows, :] = jnp.zeros((rows_blk, feats), F32)
 
     expand = w1_ref[...].reshape(feats, width)
     shrink = w2_ref[...].reshape(width, feats)
@@ -843,17 +844,13 @@
     for rows in blocks:
         act, slope = gelu_parts(dot(hidden_low[rows, :], expand, 1, 0) + shift)
         act_low = act.astype(BF16)
-        act_ref[rows, :] = act_low
+        for k in range(width // LANES):
+            column = k // parts * LANES
+            act_ref[k % parts, rows, column : column + LANES] = act_low[
+                :, k * LANES : (k + 1) * LANES
+            ]
         slope_ref[rows, :] = slope.astype(BF16)
-        part = dot(act_low, shrink, 1, 0)
-
-        @pl.when(step == 0)
-        def _():
-            resid_ref[rows, :] = part
-
-        @pl.when(step > 0)
-        def _():
-            resid_ref[rows, :] += part
+        resid_ref[rows, :] += dot(act_low, shrink, 1, 0)
 
     @pl.when(step == pl.num_programs(0) - 1)
     def _():
@@ -886,6 +883,9 @@
     rows, rows_f32 = (seq_len, feats), jax.ShapeDtypeStruct((seq_len, feats), F32)
     cols = pl.BlockSpec(rows, lambda j: (0, j))
     wide = jax.ShapeDtypeStruct((seq_len, hidden), BF16)
+    parts = w2_full.shape[1] // LANES
+    act_block = pl.BlockSpec((parts, seq_len, feats // parts), lambda j: (0, 0, j))
+    act_shape = jax.ShapeDtypeStruct((parts, seq_len, hidden // parts), BF16)
     return pl.pallas_call(
         functools.partial(feed_kernel, min(256, seq_len)),
         grid=(steps,),
@@ -896,10 +896,10 @@
             pl.BlockSpec((8 // steps, w2_full.shape[1], feats), lambda j: (j, 0, 0)),
             whole(rows, once),
         ],
-        out_specs=[cols, cols, whole(rows), whole(rows), whole(rows), whole((seq_len, LANES)),
+        out_specs=[act_block, cols, whole(rows), whole(rows), whole(rows), whole((seq_len, LANES)),
                    whole((8, feats))],
         out_shape=[
-            wide, wide, jax.ShapeDtypeStruct(rows, BF16), rows_f32, rows_f32,
+            act_shape, wide, jax.ShapeDtypeStruct(rows, BF16), rows_f32, rows_f32,
             jax.ShapeDtypeStruct((seq_len, LANES), F32), jax.ShapeDtypeStruct((8, feats), F32),
         ],
         scratch_shapes=[pltpu.VMEM(rows, BF16)],
@@ -917,26 +917,51 @@
 
     act_ref, slope_ref, w1_ref, w2_ref, resid_ref, normed_ref, inv_ref, ctx_ref = take(8)
     wo_ref, vec_ref, vec_in, out_rows = take(4)
-    d_w1, resid_out, grad_ctx, d_wo, vec_out, w2_part, out_blocks = take(7)
-    grad_ffn, hidden_low, d_w2, vec_sums = take(4)
-    count = 4
-    bufs = take(5)
-    sems = take(7)
+    d_w1, resid_out, grad_ctx, d_wo, vec_out, w2_part, w1_part, out_blocks = take(8)
+    grad_ffn, hidden_low, grad_pre, d_w2, early, vec_sums = take(6)
+    w2_bufs = take(5)
+    w2_sems = take(7)
+    w1_bufs = take(5)
+    w1_sems = take(7)
     out_sems = take(3)
 
     step = pl.program_id(0)
-    half_steps = pl.num_programs(0) // 2
+    last = pl.num_programs(0) - 1
     seq_len, feats = resid_ref.shape
-    chunk = d_w2.shape[1] // count
+    parts, chunk = d_w2.shape[0], d_w2.shape[2]
+    early_count = early.shape[0]
     place = Place(seq_size, seq_count)
     outs = RowsOut(place, out_rows, out_blocks, out_sems)
     jobs = [
         Reduce(
-            place, lambda shard, c=c: d_w2.at[shard, pl.ds(c * chunk, chunk)],
-            w2_part.at[pl.ds(c * chunk, chunk)], [buf.at[c] for buf in bufs], sems, c,
-        )
-        for c in range(count)
+            place, lambda shard, c=c: d_w2.at[c, shard], w2_part.at[pl.ds(c * chunk, chunk)],
+            [buf.at[c] for buf in w2_bufs], w2_sems, c,
+        )
+        for c in range(parts)
     ]
+    jobs += [
+        Reduce(
+            place, lambda shard, c=c: early.at[c, shard], w1_part.at[c],
+            [buf.at[c] for buf in w1_bufs], w1_sems, c,
+        )
+        for c in range(early_count)
+    ]
+    t0, t1, t2, w0, w1 = jobs
+    begin, core = Reduce.begin, Reduce.core_stage
+    one, two = Reduce.one_stage, Reduce.two_stage
+    ticks = (
+        ((begin, t0),),
+        ((begin, t1), (core, t0)),
+        ((begin, t2), (core, t1)),
+        ((one, t0), (core, t2), (begin, w0)),
+        ((one, t1), (two, t0), (core, w0), (begin, w1)),
+        ((one, t2), (two, t1), (core, w1)),
+    )
+
+    def run(stages):
+        for stage, job in stages:
+            stage(job)
+
     blocks = [pl.ds(i * rows_blk, rows_blk) for i in range(seq_len // rows_blk)]
 
     def vec(k):
@@ -950,66 +975,50 @@
         for rows in blocks:
             grad_ffn[rows, :] = resid_ref[rows, :].astype(BF16)
             hidden_low[rows, :] = (normed_ref[rows, :] * vec(G1) + vec(B1)).astype(BF16)
-
-    @pl.when(step < half_steps)
+            resid_out[rows, :] = resid_ref[rows, :]
+
+    @pl.when(step < parts)
     def _():
-        shards = 8 // half_steps
-        part = dot(act_ref[...], grad_ffn[...], 0, 0).astype(BF16)
-        d_w2[pl.ds(step * shards, shards)] = part.reshape(shards, d_w2.shape[1], feats)
-
-    @pl.when(step == half_steps - 1)
+        part = dot(act_ref[0], grad_ffn[...], 0, 0).astype(BF16)
+        d_w2[step] = part.reshape(d_w2.shape[1:])
+
+    @pl.when(step >= parts)
     def _():
-        for job in jobs:
-            job.begin()
-
-    @pl.when(step >= half_steps)
-    def _():
-        width = act_ref.shape[1]
+        width = slope_ref.shape[1]
         shrink = w2_ref[...].reshape(width, feats)
         expand = w1_ref[...].reshape(feats, width)
-        ones = jnp.ones((8, rows_blk), BF16)
-        total = jnp.zeros((8, width), F32)
-        outer = jnp.zeros((feats, width), F32)
         for rows in blocks:
             grad_act = dot(grad_ffn[rows, :], shrink, 1, 1)
-            grad_pre = (grad_act * slope_ref[rows, :].astype(F32)).astype(BF16)
-            total = total + dot(ones, grad_pre, 1, 0)
-            outer = outer + dot(hidden_low[rows, :], grad_pre, 0, 0)
-            part = dot(grad_pre, expand, 1, 1)
-
-            @pl.when(step == half_steps)
-            def _():
-                resid_out[rows, :] = resid_ref[rows, :] + part
-
-            @pl.when(step > half_steps)
-            def _():
-                resid_out[rows, :] += part
-
-        d_w1[0] = outer.astype(BF16).reshape(d_w1.shape[1:])
-        vec_sums[pl.ds(step - half_steps, 1), :] = total[0:1, :]
-
-    @pl.when(step == half_steps)
+            low = (grad_act * slope_ref[rows, :].astype(F32)).astype(BF16)
+            grad_pre[rows, :] = low
+            resid_out[rows, :] += dot(low, expand, 1, 1)
+        total = dot(jnp.ones((8, seq_len), BF16), grad_pre[...], 1, 0)
+        outer = dot(hidden_low[...], grad_pre[...], 0, 0)
+        low = outer.astype(BF16).reshape(early.shape[1:])
+
+        @pl.when(step < parts + early_count)
+        def _():
+            early[jnp.minimum(step - parts, early_count - 1)] = low
+
+        @pl.when(step >= parts + early_count)
+        def _():
+            d_w1[0] = low
+
+        vec_sums[pl.ds(step - parts, 1), :] = total[0:1, :]
+
+    for at_step, stages in enumerate(ticks):
+
+        @pl.when(step == at_step)
+        def _():
+            run(stages)
+
+    @pl.when(step == last)
     def _():
-        for job in jobs:
-            job.core_stage()
-
-    @pl.when(step == half_steps + 1)
-    def _():
-        jobs[0].one_stage()
-        jobs[1].one_stage()
-
-    @pl.when(step == half_steps + 2)
-    def _():
-        jobs[2].one_stage()
-        jobs[3].one_stage()
-        jobs[0].two_stage()
-
-    @pl.when(step == pl.num_programs(0) - 1)
-    def _():
-        jobs[1].two_stage()
+        run(((one, w0), (two, t2)))
+        for job in jobs[:parts]:
+            job.finish()
         merge = wo_ref[...].reshape(feats, feats)
         sums = [jnp.zeros((1, feats), F32)] * 3
-        outer = jnp.zeros((feats, feats), F32)
         for rows in blocks:
             grad_hidden = resid_out[rows, :]
             normed = normed_ref[rows, :]
@@ -1017,12 +1026,12 @@
             resid_out[rows, :] = grad
             low = grad.astype(BF16)
             grad_ctx[rows, :] = dot(low, merge, 1, 1).astype(BF16)
-            outer = outer + dot(ctx_ref[rows, :], low, 0, 0)
+            grad_pre[rows, :] = low
             terms = (grad_hidden * normed, grad_hidden, low.astype(F32))
             sums = [
                 total + jnp.sum(term, axis=0, keepdims=True) for total, term in zip(sums, terms)
             ]
-        d_wo[...] = outer.astype(BF16).reshape(d_wo.shape)
+        d_wo[...] = dot(ctx_ref[...], grad_pre[...], 0, 0).astype(BF16).reshape(d_wo.shape)
         row = lax.broadcasted_iota(jnp.int32, (16, 1), 0)
         lines = sums + [vec_in[k : k + 1, :] for k in range(3)]
         lines = lines + [vec_sums[k : k + 1, :] for k in range(4)]
@@ -1031,11 +1040,7 @@
             packed = jnp.where(row == k, line, packed)
         vec_out[...] = packed.astype(BF16)
 
-        for job in jobs[:2]:
-            job.finish()
-        for job in jobs[2:]:
-            job.two_stage()
-            job.finish()
+        run(((one, w1), (two, w0), (Reduce.finish, w0), (two, w1), (Reduce.finish, w1)))
         for job in jobs:
             job.drain()
         outs.finish()
@@ -1047,7 +1052,9 @@
 ):
     seq_len, feats = ctx.shape
     shard, w2_rows = w1_full.shape[1], w2_full.shape[1]
-    steps = act.shape[1] // feats
+    steps = slope.shape[1] // feats
+    parts = act.shape[0]
+    early = 2
     blk = seq_len // seq_size
     once = pl.Buffered(1)
     any_spec = pl.BlockSpec(memory_space=pl.ANY)
@@ -1057,17 +1064,17 @@
         return pl.BlockSpec(shape, lambda j: (0,) * len(shape), pipeline_mode=mode)
 
     def first(j):
-        return jnp.minimum(j, steps - 1)
+        return jnp.minimum(j, parts - 1)
 
     def second(j):
-        return jnp.maximum(j - steps, 0)
+        return jnp.maximum(j - parts, 0)
 
     rows = (seq_len, feats)
     return pl.pallas_call(
         functools.partial(feed_back_kernel, seq_size, seq_count, min(256, seq_len)),
-        grid=(2 * steps,),
+        grid=(parts + steps,),
         in_specs=[
-            pl.BlockSpec(rows, lambda j: (0, first(j))),
+            pl.BlockSpec((1,) + act.shape[1:], lambda j: (first(j), 0, 0)),
             pl.BlockSpec(rows, lambda j: (0, second(j))),
             pl.BlockSpec((8, shard, feats), lambda j: (0, 0, second(j))),
             pl.BlockSpec((8 // steps, w2_rows, feats), lambda j: (second(j), 0, 0)),
@@ -1076,23 +1083,28 @@
             any_spec,
         ],
         out_specs=[
-            pl.BlockSpec((1, 8, shard, feats), lambda j: (second(j), 0, 0, 0)),
+            pl.BlockSpec((1, 8, shard, feats), lambda j: (jnp.maximum(j - parts - early, 0), 0, 0, 0)),
             whole(rows), whole(rows), whole(wo_full.shape), whole((16, feats)),
-            any_spec, any_spec,
+            any_spec, any_spec, any_spec,
         ],
         out_shape=[
-            jax.ShapeDtypeStruct((steps, 8, shard, feats), BF16),
+            jax.ShapeDtypeStruct((steps - early, 8, shard, feats), BF16),
             jax.ShapeDtypeStruct(rows, F32), jax.ShapeDtypeStruct(rows, BF16),
             jax.ShapeDtypeStruct(wo_full.shape, BF16), jax.ShapeDtypeStruct((16, feats), BF16),
             jax.ShapeDtypeStruct((w2_rows, feats), BF16),
+            jax.ShapeDtypeStruct((early, shard, feats), BF16),
             jax.ShapeDtypeStruct((seq_count, blk, feats), BF16),
         ],
         scratch_shapes=[
-            pltpu.VMEM(rows, BF16), pltpu.VMEM(rows, BF16), pltpu.VMEM((8, w2_rows, feats), BF16),
+            pltpu.VMEM(rows, BF16), pltpu.VMEM(rows, BF16), pltpu.VMEM(rows, BF16),
+            pltpu.VMEM((parts, 8, w2_rows // parts, feats), BF16),
+            pltpu.VMEM((early, 8, shard, feats), BF16),
             pltpu.VMEM((8, feats), F32),
         ]
-        + Reduce.scratch(4, w2_rows // 4, feats)
-        + Reduce.semaphores(4)
+        + Reduce.scratch(parts, w2_rows // parts, feats)
+        + Reduce.semaphores(parts)
+        + Reduce.scratch(early, shard, feats)
+        + Reduce.semaphores(early)
         + [dma((seq_size,)), dma((seq_count,)), dma((1,))],
         compiler_params=pltpu.CompilerParams(
             collective_id=4, has_side_effects=True, vmem_limit_bytes=VMEM_MAX
@@ -1115,17 +1127,19 @@
         return got
 
     q_ref, k_ref, v_ref, ctx_ref, grad_ref, probs_ref, vec_ref = take(7)
-    x_in, qkv_in, resid_in, d_w1, d_wo, w2_part = take(6)
+    x_in, qkv_in, resid_in, d_w1, d_wo, w2_part, w1_part = take(7)
     w2_total, w1_total, wo_total, qkv_total, vec_total, token_out = take(6)
     key_acc, value_acc, grads, x_rows, qkv_mat, resid, token_rows = take(7)
     mats, bias_rows, vec_src = take(3)
     w1_count = d_w1.shape[0]
+    early_count = w1_part.shape[0]
     mat_count = w1_count + 4
     bufs = take(5)
     (arrived,) = take(1)
     vec_bufs = take(5)
     (vec_arrived,) = take(1)
-    carried_bufs = take(4)
+    w2_bufs = take(4)
+    w1_bufs = take(4)
     sems = take(7)
     z_sems = take(2)
     load_sem, carried_sems = take(2)
@@ -1143,7 +1157,8 @@
             return lambda shard: d_wo.at[shard]
         return lambda shard: mats.at[c - w1_count - 1, shard]
 
-    totals = [w1_total.at[:, pl.ds(c * feats, feats)] for c in range(w1_count)]
+    w1_totals = [w1_total.at[:, pl.ds(c * feats, feats)] for c in range(early_count + w1_count)]
+    totals = w1_totals[early_count:]
     totals += [wo_total] + [qkv_total.at[:, pl.ds(c * feats, feats)] for c in range(3)]
     jobs = [
         Reduce(
@@ -1158,18 +1173,22 @@
             sems, mat_count, vec_arrived.at[0], z_sems,
         )
     )
-    chunk = w2_part.shape[0] // 4
-    carried = []
-    for c in range(4):
-        rows = pl.ds(c * chunk, chunk)
-        carried.append(
-            Carried(
-                place, w2_part.at[rows], w2_total.at[rows], [buf.at[c] for buf in carried_bufs],
-                z_sems, carried_sems, mat_count + 1 + c, c,
-            )
-        )
-    w0, w1, w2, w3, wo, qkv_a, qkv_b, qkv_c, vec = jobs
-    t0, t1, t2, t3 = carried
+    parts = w2_bufs[0].shape[0]
+    chunk = w2_part.shape[0] // parts
+    pieces = [
+        (w2_part.at[pl.ds(c * chunk, chunk)], w2_total.at[pl.ds(c * chunk, chunk)], w2_bufs, c)
+        for c in range(parts)
+    ]
+    pieces += [(w1_part.at[c], w1_totals[c], w1_bufs, c) for c in range(early_count)]
+    carried = [
+        Carried(
+            place, source, result, [buf.at[c] for buf in held], z_sems, carried_sems,
+            mat_count + 1 + slot, slot,
+        )
+        for slot, (source, result, held, c) in enumerate(pieces)
+    ]
+    w2, w3, wo, qkv_a, qkv_b, qkv_c, vec = jobs
+    t0, t1, t2, t3, t4 = carried
     blk = seq_len // seq_size
     loads = [
         pltpu.make_async_copy(src, dst, load_sem.at[k])
@@ -1190,31 +1209,29 @@
         job.finish()
 
     ticks = (
-        ((core, w0), (core, w1)),
-        ((core, w2), (hop1, t0)),
-        ((one, w0), (hop1, t1)),
-        ((one, w1), (core, w3), (hop1, t2), (hop2, t0)),
-        ((one, w2), (hop1, t3), (hop2, t1)),
-        ((two, w0), (two, w1), (core, wo), (hop2, t2), (end, t0)),
-        ((one, w3), (core, qkv_a), (hop2, t3), (end, t1)),
-        ((two, w2), (hop1, w0), (end, t2)),
-        ((one, wo), (hop1, w1), (end, t3)),
-        ((two, w3), (core, qkv_b), (one, qkv_a), (hop1, w2), (hop2, w0)),
-        ((two, wo), (hop2, w1)),
-        ((one, qkv_b), (hop1, w3), (hop2, w2), (end, w0)),
+        ((core, w2), (core, w3)),
+        ((core, wo), (hop1, t0)),
+        ((one, w2),),
+        ((one, w3), (hop1, t1), (hop2, t0)),
+        ((one, wo), (core, qkv_a), (hop1, t2)),
+        ((two, w2), (two, w3), (hop1, t3), (hop2, t1), (end, t0)),
+        ((two, wo), (hop2, t2)),
+        ((one, qkv_a), (hop1, t4), (hop2, t3), (end, t1)),
+        ((core, qkv_b), (two, qkv_a), (hop1, w2), (end, t2)),
+        ((hop1, w3), (hop2, t4), (end, t3)),
+        ((one, qkv_b), (hop1, wo), (hop2, w2)),
+        ((two, qkv_b), (hop1, qkv_a), (hop2, w3), (end, t4)),
     )
     after = (
-        ((two, qkv_a), (end, w1)),
-        ((core, qkv_c), (hop1, wo)),
-        ((core, vec), (two, qkv_b), (hop2, w3)),
-        ((end, w2), (hop1, qkv_a)),
+        ((hop2, wo), (end, w2)),
+        ((core, qkv_c),),
+        ((core, vec), (hop1, qkv_b), (end, w3)),
+        ((hop2, qkv_a),),
     )
     rest = (
-        (one, qkv_c), (one, vec), (hop2, wo), (hop1, qkv_b), (end, w3),
-        (two, qkv_c), (two, vec), (hop2, qkv_a), (end, wo),
-        (hop1, qkv_c), (hop1, vec), (hop2, qkv_b), (end, qkv_a),
-        (hop2, qkv_c), (hop2, vec), (end, qkv_b),
-        (end, qkv_c), (end, vec),
+        (one, qkv_c), (one, vec), (end, wo), (hop2, qkv_b), (end, qkv_a),
+        (two, qkv_c), (two, vec), (hop1, qkv_c), (hop1, vec), (end, qkv_b),
+        (hop2, qkv_c), (hop2, vec), (end, qkv_c), (end, vec),
     )
 
     @pl.when(step == 0)
@@ -1222,7 +1239,7 @@
         place.barrier()
         for job in carried:
             job.load.start()
-        for job in (w0, w1, w2, w3, wo):
+        for job in (w2, w3, wo):
             job.begin()
         for load in loads:
             load.start()
@@ -1307,14 +1324,15 @@
 
 def backward_all(
     seq_size, seq_count, query, key, value, ctx, grad_ctx, probs, vecs, inputs, qkv_full, resid,
-    d_w1, d_wo, w2_part,
+    d_w1, d_wo, w2_part, w1_part,
 ):
     seq_len, feats = ctx.shape
     blk = seq_len // seq_size
     shard = qkv_full.shape[1]
     w1_count = d_w1.shape[0]
+    early = w1_part.shape[0]
     count = w1_count + 4
-    chunk = w2_part.shape[0] // 4
+    parts = w2_part.shape[0] // LANES
     any_spec = pl.BlockSpec(memory_space=pl.ANY)
     cols = pl.BlockSpec((seq_len, LANES), lambda g: (0, g))
     dma = pltpu.SemaphoreType.DMA
@@ -1330,10 +1348,10 @@
             pl.BlockSpec((2, seq_len, seq_len), lambda g: (g, 0, 0)),
             pl.BlockSpec(vecs.shape, lambda g: (0, 0)),
         ]
-        + [any_spec] * 6,
+        + [any_spec] * 7,
         out_specs=[any_spec] * 6,
         out_shape=[
-            low(*w2_part.shape), low(shard, w1_count * feats), low(shard, feats),
+            low(*w2_part.shape), low(shard, (early + w1_count) * feats), low(shard, feats),
             low(shard, 3 * feats), low(32, feats), low(seq_count, blk, feats),
         ],
         scratch_shapes=[pltpu.VMEM((2, HEAD, seq_len), F32)] * 2
@@ -1352,17 +1370,18 @@
         + Reduce.scratch(1, 32, feats)
         + [pltpu.VMEM((1, 2, 32, feats), BF16)]
         + [
-            pltpu.VMEM((4, chunk, feats), BF16), pltpu.VMEM((4, 2, chunk, feats), BF16),
-            pltpu.VMEM((4, 2, chunk, feats), BF16), pltpu.VMEM((4, chunk, feats), BF16),
+            pltpu.VMEM((parts,) + lead + (LANES, feats), BF16) for lead in ((), (2,), (2,), ())
         ]
+        + [pltpu.VMEM((early,) + lead + (shard, feats), BF16) for lead in ((), (2,), (2,), ())]
         + Reduce.semaphores(count + 1)
-        + Chain.semaphores(count + 5)
-        + [dma((3,)), dma((4, 2)), dma((seq_size,)), dma((seq_count,)), dma((1,))],
+        + Chain.semaphores(count + 1 + parts + early)
+        + [dma((3,)), dma((parts + early, 2)), dma((seq_size,)), dma((seq_count,)), dma((1,))],
         compiler_params=pltpu.CompilerParams(
             collective_id=1, has_side_effects=True, vmem_limit_bytes=VMEM_MAX
         ),
     )(
-        query, key, value, ctx, grad_ctx, probs, vecs, inputs, qkv_full, resid, d_w1, d_wo, w2_part
+        query, key, value, ctx, grad_ctx, probs, vecs, inputs, qkv_full, resid, d_w1, d_wo,
+        w2_part, w1_part,
     )
 
 
@@ -1501,13 +1520,13 @@
         act, slope, out_rows, grad_resid2, normed1, inv1, second_sums = feed_forward(
             ctx, inputs, wo_full, vec_rows, w1_full, w2_full, dy
         )
-        d_w1, grad_resid1, grad_ctx, d_wo, vec_sums, part_w2, output = feed_back(
+        d_w1, grad_resid1, grad_ctx, d_wo, vec_sums, part_w2, part_w1, output = feed_back(
             seq_size, seq_count, act, slope, w1_full, w2_full, grad_resid2, normed1, inv1, ctx,
             wo_full, vec_rows, second_sums, out_rows,
         )
         *sums, token_grad = backward_all(
             seq_size, seq_count, query, key, value, ctx, grad_ctx, probs, vec_sums, inputs,
-            qkv_full, grad_resid1, d_w1, d_wo, part_w2,
+            qkv_full, grad_resid1, d_w1, d_wo, part_w2, part_w1,
         )
         sum_w2, sum_w1, s_wo, s_wq, s_wk, s_wv, *vec_sums = widen(*sums)
         vec_sums = [item.reshape(-1) for item in vec_sums]

time: 279 us -> 262 us (0.939); the launches traced: 274 us -> 262 us
  Pallas kernels: 268 us -> 256 us
    pallas_call x1, Pallas kernels: 30.4 us -> 26.3 us  [feed_forward(): pl.pallas_call(functools.partial(feed_kernel, min(256, seq_len)), grid=(s...]
    pallas_call x1, Pallas kernels: 98.1 us -> 94 us  [backward_all(): pl.pallas_call(functools.partial(backward_kernel, seq_size, seq_count, se...]
    pallas_call x1, Pallas kernels: 54.3 us -> 50.6 us  [feed_back(): pl.pallas_call(functools.partial(feed_back_kernel, seq_size, seq_count, m...]
where the time goes in v2:
time: 262 us
  Pallas kernels  256 us (98%)
  local copies, waits for them, and re-layouts  3.28 us (1%)
    pallas_call x1, Pallas kernels, backward_all(): pl.pallas_call(functools.partial(backward_kernel, seq_size, seq_count, se...  94 us
    pallas_call x1, Pallas kernels, feed_back(): pl.pallas_call(functools.partial(feed_back_kernel, seq_size, seq_count, m...  50.6 us
    pallas_call x1, Pallas kernels, forward_all(): pl.pallas_call(functools.partial(forward_kernel, seq_size, seq_count, min...  42.4 us
    pallas_call x1, Pallas kernels, start_all(): pl.pallas_call(functools.partial(start_kernel, seq_size, seq_count), in_s...  39.3 us
    pallas_call x1, Pallas kernels, feed_forward(): pl.pallas_call(functools.partial(feed_kernel, min(256, seq_len)), grid=(s...  26.3 us

profile of v2, /device:TPU:0, one launch (start us, length us, event | category | flops | bytes accessed | tf_op | source)
XLA Modules:
  0.0 261.8 jit_solution(12521387844852366078)
XLA Ops:
  0.7 1.2 reshape.96.refs_8_
  1.9 39.3 %shard_map.305 = (bf16[1024,768]{1,0:T(8,128)(2,1)}, bf16[8,96,2304]{2,1,0:T(8,128)(2,1)}, bf16[8,32,128]{2,1,0:T(8,128)(2,1)}, bf16[8,384,768]{2,1,0:T(8,128)(2...) custom-call(bf16[3,256,768]{2,1,0:T(8,128)(2,1)} %tokens.1, f32[96,768]{1,0:T(8,128)} %wq.1, ...), custom_call_target="tpu_custom_call" | custom-call | tf_op jit(solution)/shard_map/pallas_call | solution.py:366
  41.2 42.4 %shard_map.306 = (bf16[1024,768]{1,0:T(8,128)(2,1)}, bf16[1024,768]{1,0:T(8,128)(2,1)}, bf16[1024,768]{1,0:T(8,128)(2,1)}, bf16[1024,768]{1,0:T(8,128)(2,1)}, bf...) custom-call(s32[3]{0:T(128)} %len_ref.1, ...), custom_call_target="tpu_custom_call", output_to_operand_aliasing={{7}: (7, {}), {8}: (8, {}), {9}: (9, {})} | custom-call | tf_op jit(solution)/shard_map/pallas_call | solution.py:483
  83.5 26.3 %shard_map.307 = (bf16[3,1024,1024]{2,1,0:T(8,128)(2,1)}, bf16[1024,3072]{1,0:T(8,128)(2,1)}, bf16[1024,768]{1,0:T(8,128)(2,1)}, f32[1024,768]{1,0:T(8,128)}, f3...) custom-call(bf16[1024,768]{1,0:T(8,128)(2,1)} %get-tuple-element.75.ctx_ref.refs_7_.refs_3_, ...), custom_call_target="tpu_custom_call" | custom-call | tf_op jit(solution)/shard_map/pallas_call | solution.py:889
  109.8 50.6 %shard_map.308 = (bf16[2,8,96,768]{3,2,1,0:T(8,128)(2,1)}, f32[1024,768]{1,0:T(8,128)}, bf16[1024,768]{1,0:T(8,128)(2,1)}, bf16[8,96,768]{2,1,0:T(8,128)(2,1)}, ...) custom-call(bf16[3,1024,1024]{2,1,0:T(8,128)(2,1)} %get-tuple-elemen, ...), custom_call_target="tpu_custom_call" | custom-call | tf_op jit(solution)/shard_map/pallas_call | solution.py:1073
  160.4 94.0 %shard_map.309 = (bf16[384,768]{1,0:T(8,128)(2,1)}, bf16[96,3072]{1,0:T(8,128)(2,1)}, bf16[96,768]{1,0:T(8,128)(2,1)}, bf16[96,2304]{1,0:T(8,128)(2,1)}, bf16[32...) custom-call(bf16[1024,768]{1,0:T(8,128)(2,1)} %get-tuple-element.89.refs_0_, bf16[1024,768]{1,0:T(8,128)(2,1)} %get-tuple-element.90.refs_1_, ...), custom_call_target="tpu_custom_call" | custom-call | tf_op jit(solution)/shard_map/pallas_call | solution.py:1343
  254.5 0.0 copy-start
  254.5 3.9 %shard_map.310 = (f32[384,768]{1,0:T(8,128)}, f32[96,3072]{1,0:T(8,128)}, f32[96,768]{1,0:T(8,128)}, f32[96,768]{1,0:T(8,128)}, f32[96,768]{1,0:T(8,128)}, /*ind...) custom-call(bf16[384,768]{1,0:T(8,128)(2,1)} %get-tuple-element.101., ...), custom_call_target="tpu_custom_call" | custom-call | tf_op jit(solution)/shard_map/pallas_call | solution.py:1420
  258.4 0.0 copy-start.1
  258.4 1.4 reduce
  259.8 0.0 copy-done
  259.8 1.0 copy.43
  260.8 0.0 copy-done.1
  260.8 1.0 copy.44
Async XLA Ops:
  254.5 5.3 %copy-start = (bf16[3,256,768]{2,1,0:T(8,128)(2,1)S(1)}, bf16[3,256,768]{2,1,0:T(8,128)(2,1)}, u32[]{:S(2)}) copy-start(bf16[3,256,768]{2,1,0:T(8,128)(2,1)} %get-tuple-element.138) | copy-start | bytes 3538948
  258.4 2.4 copy-start.1
